TPU v7x, 256 devices: a whole 4x4x8 slice. The times are simulated.
256 devices in a mesh: date: 16 (over x, y_hi, core), rng: 16 (over z, y_lo).
Axes of the slice: x: 4, y: 4 (y_hi: 2, y_lo: 2; y = y_hi * 2 + y_lo), z: 8, core: 2. Of those that a mesh axis runs over, the one named last changes fastest.
Arguments:
- slave_complex_pixels: bfloat16 [32, 2, 128, 4096], P(None, None, 'date', 'rng')
- along_track_line_groups: int32 [32, 16, 64], P(None, 'rng'), may hold values from 0 to 126, as said below
- master_epoch_position: int32 [1], replicated, may hold values from 0 to 31
- sweep_identifier: int32 [64], replicated, may hold values from 0 to 1, never falling along the last dimension, each value on 1 to 48 neighbouring positions
- initial_filter_kernel: float32 [32, 5, 3, 3], replicated, may hold values from -0.875 to 0.875
- initial_filter_shift: float32 [32], replicated, may hold values from -3 to 3
- latter_filter_kernel: float32 [2, 32, 3, 3], replicated, may hold values from -0.375 to 0.375
- latter_filter_shift: float32 [2], replicated, may hold values from -3 to 3
Outputs:
- burn_logits: float32 [32, 2, 64, 4096], P('date', None, None, 'rng')
Inputs may be any that keep to these rules, and one draw needn't show every extreme that they name: along_track_line_groups[d, g] is strictly increasing: the ingested rows that give the 64 window rows of date d in range segment g. `sweep_identifier`: burst never falls along the rows; each burst holds between 16 and 48 rows.
All inputs are finite; a program needn't handle non-finite values.
Results may differ from a plain program's by a relative error of at most 0.0003.
Values may be sent and summed in bfloat16 or wider, within the bound.
No kernel may reach another device: no remote copies, remote signals or barrier semaphores. Data moves between devices by JAX's collectives and lax.ppermute only.
A program may use at most 128 MiB of HBM per device.

v0:
```python
import jax
import jax.numpy as jnp
from jax import lax
from jax.sharding import PartitionSpec as P

BOX_AZ = 7
BOX_RG = 28


HIGH = lax.Precision.HIGHEST
EPSILON = 1e-06


def from_root(shard, axis, root):
    mine = lax.axis_index(axis) == root
    return lax.psum(jnp.where(mine, shard, jnp.zeros_like(shard)), axis)


def extended(shard, sides, width):
    for axis, dim in sides:
        devices, length = (lax.axis_size(axis), shard.shape[dim])
        up = [(i, (i + 1) % devices) for i in range(devices - 1)]
        down = [(j, i) for i, j in up]
        last = lax.slice_in_dim(shard, length - width, length, axis=dim)
        first = lax.slice_in_dim(shard, 0, width, axis=dim)
        before = lax.ppermute(last, axis, up)
        after = lax.ppermute(first, axis, down)
        shard = jnp.concatenate([before, shard, after], axis=dim)
    return shard


def pick_rows(one_frame, row_index):
    return jnp.take(one_frame, row_index, axis=1)


def features(moving_averaged):
    denominator = jnp.sqrt(moving_averaged[0] * moving_averaged[1]) + EPSILON
    return jnp.stack(
        [
            moving_averaged[2] / denominator,
            moving_averaged[3] / denominator,
            moving_averaged[4] / denominator,
            jnp.log(moving_averaged[1] + EPSILON) - jnp.log(moving_averaged[0] + EPSILON),
            jnp.log(moving_averaged[0] / (BOX_AZ * BOX_RG) + EPSILON),
        ]
    )


def range_band(padded_cols, result_across_lines):
    source_col = lax.broadcasted_iota(jnp.int32, (padded_cols, result_across_lines), 0)
    target_col = lax.broadcasted_iota(jnp.int32, (padded_cols, result_across_lines), 1)
    line_displacement = source_col - target_col
    return ((line_displacement >= 0) & (line_displacement < BOX_RG)).astype(jnp.float32)


def along_track_line_blocks(slant_averaged, sweep_identifier):
    along_track_lines_number = sweep_identifier.shape[0]
    block_line_number = min(128, along_track_lines_number)
    midway_line_number = (BOX_AZ - 1) // 2
    bordered_patch = jnp.pad(
        slant_averaged, ((0, 0), (0, 0), (midway_line_number, midway_line_number), (0, 0))
    )
    sweep_border_fill = jnp.pad(
        sweep_identifier, (midway_line_number, midway_line_number), constant_values=-1
    )
    patch_line_extent = block_line_number + 2 * midway_line_number
    target_row = lax.broadcasted_iota(jnp.int32, (block_line_number, patch_line_extent), 0)
    source_row = lax.broadcasted_iota(jnp.int32, (block_line_number, patch_line_extent), 1)
    near_rows = jnp.abs(source_row - midway_line_number - target_row) <= midway_line_number
    band_rows = (near_rows & (sweep_identifier[:, None] == sweep_border_fill[None, :])).astype(
        jnp.float32
    )
    results = jnp.einsum("pq,knqb->knpb", band_rows, bordered_patch, precision=HIGH)
    return results


def moving_average_planes(bordered_patch, sweep_identifier, result_across_lines):
    as_float = bordered_patch.astype(jnp.float32)
    ref_re = as_float[0, 0]
    ref_im = as_float[0, 1]
    sec_re = as_float[1:, 0]
    sec_im = as_float[1:, 1]
    pow_ref = jnp.broadcast_to(ref_re * ref_re + ref_im * ref_im, sec_re.shape)
    pow_sec = sec_re * sec_re + sec_im * sec_im
    cross_re = ref_re * sec_re + ref_im * sec_im
    cross_im = ref_im * sec_re - ref_re * sec_im
    layered_planes = jnp.stack([pow_ref, pow_sec, cross_re, cross_im, jnp.sqrt(pow_ref * pow_sec)])
    slant_averaged = jnp.einsum(
        "knpa,ab->knpb",
        layered_planes,
        range_band(bordered_patch.shape[3], result_across_lines),
        precision=HIGH,
    )
    moving_averaged = along_track_line_blocks(slant_averaged, sweep_identifier)
    return features(moving_averaged)


def conv_taps(field, weights, biases):
    along_track_lines_number = field.shape[2]
    across_track_number = field.shape[3] - 2
    bordered_patch = jnp.pad(field, ((0, 0), (0, 0), (1, 1), (0, 0)))
    cumulative_tally = (
        jnp.zeros(
            (weights.shape[0], field.shape[1], along_track_lines_number, across_track_number),
            jnp.float32,
        )
        + biases[:, None, None, None]
    )
    for tap_a in range(3):
        for tap_b in range(3):
            cumulative_tally = cumulative_tally + jnp.einsum(
                "oi,inpw->onpw",
                weights[:, :, tap_a, tap_b],
                bordered_patch[
                    :,
                    :,
                    tap_a : tap_a + along_track_lines_number,
                    tap_b : tap_b + across_track_number,
                ],
                precision=HIGH,
            )
    return cumulative_tally


def local(
    slave_complex_pixels,
    along_track_line_groups,
    master_epoch_position,
    sweep_identifier,
    initial_filter_kernel,
    initial_filter_shift,
    latter_filter_kernel,
    latter_filter_shift,
):
    date_count = lax.axis_size("date")
    date_index = lax.axis_index("date")
    per_dev = slave_complex_pixels.shape[0] // date_count
    across_track_number = slave_complex_pixels.shape[3]
    chosen = master_epoch_position[0]
    my_lists = along_track_line_groups[:, 0, :]
    lists_here = lax.dynamic_slice_in_dim(my_lists, date_index * per_dev, per_dev, 0)
    arrived = lax.all_to_all(slave_complex_pixels, "date", split_axis=0, concat_axis=2, tiled=True)
    secondary = jax.vmap(pick_rows)(arrived, lists_here)
    local_ref = lax.dynamic_index_in_dim(secondary, chosen % per_dev, 0, keepdims=False)
    ref_frame = from_root(local_ref, "date", chosen // per_dev)
    stacked = jnp.concatenate([ref_frame[None], secondary], 0)
    bordered_patch = extended(stacked, (("rng", 3),), BOX_RG // 2)
    descriptor_lattice = moving_average_planes(
        bordered_patch, sweep_identifier, across_track_number
    )
    descriptor_lattice = extended(descriptor_lattice, (("rng", 3),), 1)
    hidden = jax.nn.relu(conv_taps(descriptor_lattice, initial_filter_kernel, initial_filter_shift))
    hidden = extended(hidden, (("rng", 3),), 1)
    burn_logits = conv_taps(hidden, latter_filter_kernel, latter_filter_shift)
    return jnp.moveaxis(burn_logits, 0, 1)


def solution(mesh):
    placed = (P(None, None, "date", "rng"), P(None, "rng", None), P(), P(), P(), P(), P(), P())
    return jax.shard_map(
        local, mesh=mesh, in_specs=placed, out_specs=P("date", None, None, "rng"), check_vma=False
    )
```

profile of v0, /device:TPU:128, one launch (start us, length us, event | category | flops | bytes accessed | tf_op | source)
XLA Modules:
  0.0 294.7 jit_solution(7778671245150096637)
XLA Ops:
  6.5 7.2 %all-to-all-start = ((bf16[32,2,8,256]{3,2,1,0:T(8,128)(2,1)}), bf16[32,2,8,256]{3,2,1,0:T(8,128)(2,1)S(1)}, u32[]{:S(2)}, u32[]{:S(2)}) async-start(bf16[32,2,8,256]{3,2,1,0:T(8,128)(2,1)} %param.8), calls=%async_computation | async-start | bytes 524288 | tf_op jit(solution)/shard_map/all_to_all | solution.py:142
  13.7 0.0 all-reduce.6.cloned.1.call-start
  14.5 0.1 reshape.128
  14.6 0.9 fusion.117
  15.5 7.4 %all-to-all-done = bf16[32,2,8,256]{3,2,1,0:T(8,128)(2,1)S(1)} async-done(((bf16[32,2,8,256]{3,2,1,0:T(8,128)(2,1)}), bf16[32,2,8,256]{3,2,1,0:T(8,128)(2,1)S(1)}, u32[]{:S(2)}, u32[]{:S(2)}) %all-to-all-start) | async-done | bytes 262176 | tf_op jit(solution)/shard_map/all_to_all | solution.py:142
  22.9 0.3 copy.74
  23.2 1.0 gather_fusion
  24.2 0.1 broadcast_select_fusion
  24.3 0.6 select_bitcast_fusion
  25.0 0.0 all-reduce.6.cloned.1.call-update
  25.0 0.1 fusion.120
  25.1 131.5 %all-reduce.6.cloned.1.call-done = bf16[1,2,64,256]{3,2,0,1:T(8,128)(2,1)} async-done(((bf16[1,2,64,256]{3,2,0,1:T(8,128)(2,1)}), bf16[1,2,64,256]{3,2,0,1:T(8,128)(2,1)}) %all-reduce.6.cloned.1.call-update) | async-done | bytes 65552 | tf_op jit(solution)/shard_map/psum | solution.py:16
  156.6 0.9 fusion.77
  157.4 3.4 %collective-permute-start = (bf16[3,2,64,14]{3,2,0,1:T(8,128)(2,1)S(1)}, bf16[3,2,64,14]{3,2,0,1:T(8,128)(2,1)S(1)}, u32[]{:S(2)}, u32[]{:S(2)}) collective-permute-start(bf16[3,2,64,14]{3,2,0,1:T(8,128)(2,1)S(1)} %get-tuple-element.23), channel_id=1, source_target_pairs={{0,1},{1,2},{2,3},{3,4},{4,5},{5,6},{6,7},{7,8},{8,9},{9,10},{10,1... | collective-permute-start | bytes 32264 | tf_op jit(solution)/shard_map/ppermute | solution.py:26
  160.8 4.6 %collective-permute-start.1 = (bf16[3,2,64,14]{3,2,0,1:T(8,128)(2,1)S(1)}, bf16[3,2,64,14]{3,2,0,1:T(8,128)(2,1)S(1)}, u32[]{:S(2)}, u32[]{:S(2)}) collective-permute-start(bf16[3,2,64,14]{3,2,0,1:T(8,128)(2,1)S(1)} %get-tuple-element.24), channel_id=1, source_target_pairs={{1,0},{2,1},{3,2},{4,3},{5,4},{6,5},{7,6},{8,7},{9,8},{10,9},{11,1... | collective-permute-start | bytes 32264 | tf_op jit(solution)/shard_map/ppermute | solution.py:27
  165.4 0.7 pad.17
  166.1 1.4 collective-permute-done.1
  167.6 0.9 multiply_add_fusion
  168.5 0.1 fusion.71
  168.7 0.1 sqrt_dynamic-update-slice_fusion
  168.8 0.7 fusion.60
  169.6 0.6 convolution_bitcast_fusion
  170.1 0.1 fusion.76
  170.2 0.1 fusion.75
  170.3 0.1 fusion.74
  170.4 0.2 fusion.116
  170.6 3.2 %collective-permute-start.2 = (f32[5,2,64,1]{3,2,1,0:T(8,128)S(1)}, f32[5,2,64,1]{3,2,1,0:T(8,128)S(1)}, u32[]{:S(2)}, u32[]{:S(2)}) collective-permute-start(f32[5,2,64,1]{3,2,1,0:T(8,128)S(1)} %get-tuple-element.21), channel_id=1, source_target_pairs={{0,1},{1,2},{2,3},{3,4},{4,5},{5,6},{6,7},{7,8},{8,9},{9,10},{10,1... | collective-permute-start | bytes 7688 | tf_op jit(solution)/shard_map/ppermute | solution.py:26
  173.8 5.3 %collective-permute-start.3 = (f32[5,2,64,1]{3,2,1,0:T(8,128)S(1)}, f32[5,2,64,1]{3,2,1,0:T(8,128)S(1)}, u32[]{:S(2)}, u32[]{:S(2)}) collective-permute-start(f32[5,2,64,1]{3,2,1,0:T(8,128)S(1)} %get-tuple-element.22), channel_id=1, source_target_pairs={{1,0},{2,1},{3,2},{4,3},{5,4},{6,5},{7,6},{8,7},{9,8},{10,9},{11,1... | collective-permute-start | bytes 7688 | tf_op jit(solution)/shard_map/ppermute | solution.py:27
  179.1 3.6 %fusion.45 = f32[2,64,256,32]{2,3,1,0:T(8,128)S(1)} fusion(f32[5,2,64,256]{3,2,1,0:T(8,128)S(1)} %log_dynamic-update-slice_fusion, f32[32,5,1,1]{0,3,2,1:T(1,128)S(1)} %get-tuple-element.28), kind=kOutput, calls=%fused_computation.48 | convolution fusion | flops 62914560 | bytes 4850304 | tf_op jit(solution)/shard_map/oi,inpw->onpw/dot_general | solution.py:111
  182.7 2.1 collective-permute-done.2
  184.8 3.9 %collective-permute-done.3 = f32[5,2,64,1]{3,2,1,0:T(8,128)S(1)} collective-permute-done((f32[5,2,64,1]{3,2,1,0:T(8,128)S(1)}, f32[5,2,64,1]{3,2,1,0:T(8,128)S(1)}, u32[]{:S(2)}, u32[]{:S(2)}) %collective-permute-start.3) | collective-permute-done | bytes 2592 | tf_op jit(solution)/shard_map/ppermute | solution.py:27
  188.7 0.5 select_maximum_fusion.2
  189.2 0.8 fusion.115
  190.0 3.6 %fusion.53 = f32[2,64,256,32]{2,3,1,0:T(8,128)S(1)} fusion(f32[5,2,64,256]{3,2,1,0:T(8,128)S(1)} %get-tuple-element.13, f32[32,5,1,1]{0,3,2,1:T(1,128)S(1)} %get-tuple-element.32), kind=kOutput, calls=%fused_computation.56 | convolution fusion | flops 62914560 | bytes 4850304 | tf_op jit(solution)/shard_map/oi,inpw->onpw/dot_general | solution.py:111
  193.5 3.6 %fusion.40 = f32[2,64,256,32]{2,3,1,0:T(8,128)S(1)} fusion(f32[5,2,64,256]{3,2,1,0:T(8,128)S(1)} %get-tuple-element.14, f32[32,5,1,1]{0,3,2,1:T(1,128)S(1)} %get-tuple-element.26), kind=kOutput, calls=%fused_computation.43 | convolution fusion | flops 62914560 | bytes 4850304 | tf_op jit(solution)/shard_map/oi,inpw->onpw/dot_general | solution.py:111
  197.1 5.3 %fusion.42 = f32[2,64,256,32]{2,3,1,0:T(8,128)} fusion(f32[5,2,64,256]{3,2,1,0:T(8,128)S(1)} %get-tuple-element.15, f32[32,5,1,1]{0,3,2,1:T(1,128)S(1)} %get-tuple-element.27), kind=kOutput, calls=%fused_computation.45 | convolution fusion | flops 62914560 | bytes 4850304 | tf_op jit(solution)/shard_map/oi,inpw->onpw/dot_general | solution.py:111
  202.4 5.0 %fusion.49 = f32[2,64,256,32]{2,3,1,0:T(8,128)} fusion(f32[5,2,64,256]{3,2,1,0:T(8,128)S(1)} %get-tuple-element.16, f32[32,5,1,1]{0,3,2,1:T(1,128)S(1)} %get-tuple-element.30), kind=kOutput, calls=%fused_computation.52 | convolution fusion | flops 62914560 | bytes 4850304 | tf_op jit(solution)/shard_map/oi,inpw->onpw/dot_general | solution.py:111
  207.5 5.1 %fusion.51 = f32[2,64,256,32]{2,3,1,0:T(8,128)} fusion(f32[5,2,64,256]{3,2,1,0:T(8,128)S(1)} %get-tuple-element.17, f32[32,5,1,1]{0,3,2,1:T(1,128)S(1)} %get-tuple-element.31), kind=kOutput, calls=%fused_computation.54 | convolution fusion | flops 62914560 | bytes 4850304 | tf_op jit(solution)/shard_map/oi,inpw->onpw/dot_general | solution.py:111
  212.5 5.0 %fusion.38 = f32[2,64,256,32]{2,3,1,0:T(8,128)} fusion(f32[5,2,64,256]{3,2,1,0:T(8,128)S(1)} %get-tuple-element.18, f32[32,5,1,1]{0,3,2,1:T(1,128)S(1)} %get-tuple-element.33), kind=kOutput, calls=%fused_computation.41 | convolution fusion | flops 62914560 | bytes 4850304 | tf_op jit(solution)/shard_map/oi,inpw->onpw/dot_general | solution.py:111
  217.6 0.5 pad_maximum_fusion.14
  218.1 5.0 %fusion.47 = f32[2,64,256,32]{2,3,1,0:T(8,128)} fusion(f32[5,2,64,256]{3,2,1,0:T(8,128)S(1)} %get-tuple-element.20, f32[32,5,1,1]{0,3,2,1:T(1,128)S(1)} %get-tuple-element.29), kind=kOutput, calls=%fused_computation.50 | convolution fusion | flops 62914560 | bytes 4850304 | tf_op jit(solution)/shard_map/oi,inpw->onpw/dot_general | solution.py:111
  223.1 10.2 %maximum_bitcast_fusion = f32[32,2,64,256]{3,0,2,1:T(8,128)S(1)} fusion(f32[2,64,256,32]{2,3,1,0:T(8,128)} %fusion.38, f32[2,64,256,32]{2,3,1,0:T(8,128)S(1)} %fusion.40, f32[2,64,256,32]{2,3,1,0:T(8,128)} %fusion.42, f32[2,64,256,32]{2,3,1,0:T(8,128)S(1)} %fusion.45, f32[2,64,256,32]{2,3,1,0:T(8,128)} %fusion.47, f32[2,64,256,32]{2,3,1,0:T(8,128)} %fusion.49, ...), kind=kOutput, calls=%fused_computation.24 | convolution fusion | flops 73400320 | bytes 38404864 | tf_op jit(solution)/shard_map/oi,inpw->onpw/dot_general | solution.py:111
  233.3 0.0 copy-start.6
  233.3 3.2 %fusion.114 = (f32[32,2,64,1]{3,0,2,1:T(8,128)}, f32[32,2,64,1]{3,0,2,1:T(8,128)}) fusion(f32[32,2,64,256]{3,0,2,1:T(8,128)S(1)} %maximum_bitcast_fusion), kind=kLoop, calls=%fused_computation.148 | loop fusion | bytes 65536 | tf_op jit(solution)/shard_map/slice | solution.py:24
  236.5 0.1 copy-done.2
  236.6 2.8 copy.95
  239.4 2.3 collective-permute-start.4
  241.7 4.5 %fusion.102 = f32[2,64,256,2]{2,3,1,0:T(2,128)S(1)} fusion(f32[32,2,64,256]{3,0,2,1:T(8,128)} %copy-done.2, f32[2,32,3,3]{1,0,3,2:T(2,128)S(1)} %copy-done.6), kind=kOutput, calls=%fused_computation.134 | convolution fusion | flops 25165824 | bytes 4457472 | tf_op jit(solution)/shard_map/oi,inpw->onpw/dot_general | solution.py:111
  246.2 1.1 copy.96
  247.3 6.0 %collective-permute-start.5 = (f32[32,2,64,1]{2,0,3,1:T(8,128)S(1)}, f32[32,2,64,1]{2,0,3,1:T(8,128)S(1)}, u32[]{:S(2)}, u32[]{:S(2)}) collective-permute-start(f32[32,2,64,1]{2,0,3,1:T(8,128)S(1)} %copy.96), channel_id=1, source_target_pairs={{1,0},{2,1},{3,2},{4,3},{5,4},{6,5},{7,6},{8,7},{9,8},{10,9},{11,1... | collective-permute-start | bytes 49160 | tf_op jit(solution)/shard_map/ppermute | solution.py:27
  253.4 1.9 copy.97
  255.2 4.9 %fusion.9 = f32[2,64,256,2]{2,3,1,0:T(2,128)S(1)} fusion(f32[32,2,64,256]{3,0,2,1:T(8,128)} %copy-done.2, f32[32,2,64,1]{3,0,2,1:T(8,128)S(1)} %copy.97, f32[2,32,3,3]{1,0,3,2:T(2,128)S(1)} %copy-done.6), kind=kOutput, calls=%fused_computation.16 | convolution fusion | flops 26214400 | bytes 6554624 | tf_op jit(solution)/shard_map/oi,inpw->onpw/dot_general | solution.py:111
  260.1 2.9 copy.98
  263.1 5.0 %select_maximum_fusion = f32[32,2,66,258]{3,0,2,1:T(8,128)S(1)} fusion(f32[32,2,64,1]{3,0,2,1:T(8,128)} %copy.98, f32[32,2,64,256]{3,0,2,1:T(8,128)} %copy-done.2, f32[32,2,64,1]{3,0,2,1:T(8,128)S(1)} %copy.97), kind=kLoop, calls=%fused_computation.3 | loop fusion | flops 8718336 | bytes 8586240 | tf_op jit(solution)/shard_map/concatenate | solution.py:28
  268.0 2.6 fusion.3
  270.7 2.3 fusion.5
  273.0 2.6 fusion.11
  275.6 0.0 copy-start.8
  275.6 2.6 fusion.13
  278.3 2.9 fusion.1
  281.2 0.0 copy-start.1
  281.2 2.4 fusion.34
  283.6 3.3 %fusion.27 = f32[2,2,64,256]{3,1,2,0:T(2,128)S(1)} fusion(f32[2,64,256,2]{2,3,1,0:T(2,128)S(1)} %fusion.1, f32[2,64,256,2]{2,3,1,0:T(2,128)S(1)} %fusion.3, f32[2,64,256,2]{2,3,1,0:T(2,128)S(1)} %fusion.5, f32[2,64,256,2]{2,3,1,0:T(2,128)S(1)} %fusion.34, f32[32,2,64,1]{3,0,2,1:T(8,128)S(1)} %copy-done.4, f32[32,2,64,256]{3,0,2,1:T(8,128)S(1)} %copy-done.3, ...), kind=kOutput, calls=%fused_computation.34 | convolution fusion | flops 26476544 | bytes 7603200 | tf_op jit(solution)/shard_map/oi,inpw->onpw/dot_general | solution.py:111
  286.9 0.7 copy.101
  (30 shorter events, 0.3 us)
Async XLA Ops:
  6.5 7.2 %copy-start = (s32[32,1,64]{2,1,0:T(1,128)S(1)}, s32[32,1,64]{2,1,0:T(1,128)}, u32[]{:S(2)}) copy-start(s32[32,1,64]{2,1,0:T(1,128)} %param.9) | copy-start | bytes 24580
  6.5 163.0 %copy-start.9 = (s32[64]{0:T(128)S(1)}, s32[64]{0:T(128)}, u32[]{:S(2)}) copy-start(s32[64]{0:T(128)} %param.11) | copy-start | bytes 772
  6.5 16.3 %all-to-all-start = ((bf16[32,2,8,256]{3,2,1,0:T(8,128)(2,1)}), bf16[32,2,8,256]{3,2,1,0:T(8,128)(2,1)S(1)}, u32[]{:S(2)}, u32[]{:S(2)}) async-start(bf16[32,2,8,256]{3,2,1,0:T(8,128)(2,1)} %param.8), calls=%async_computation | async-start | bytes 524288 | tf_op jit(solution)/shard_map/all_to_all | solution.py:142
  13.7 142.8 %all-reduce.6.cloned.1.call-start = ((), (), s32[]{:S(2)}) async-start(), calls=%async_computation.1 | async-start | bytes 131072 | tf_op jit(solution)/shard_map/psum | solution.py:16
  157.4 8.7 %collective-permute-start = (bf16[3,2,64,14]{3,2,0,1:T(8,128)(2,1)S(1)}, bf16[3,2,64,14]{3,2,0,1:T(8,128)(2,1)S(1)}, u32[]{:S(2)}, u32[]{:S(2)}) collective-permute-start(bf16[3,2,64,14]{3,2,0,1:T(8,128)(2,1)S(1)} %get-tuple-element.23), channel_id=1, source_target_pairs={{0,1},{1,2},{2,3},{3,4},{4,5},{5,6},{6,7},{7,8},{8,9},{9,10},{10,1... | collective-permute-start | bytes 32264 | tf_op jit(solution)/shard_map/ppermute | solution.py:26
  160.8 6.8 %collective-permute-start.1 = (bf16[3,2,64,14]{3,2,0,1:T(8,128)(2,1)S(1)}, bf16[3,2,64,14]{3,2,0,1:T(8,128)(2,1)S(1)}, u32[]{:S(2)}, u32[]{:S(2)}) collective-permute-start(bf16[3,2,64,14]{3,2,0,1:T(8,128)(2,1)S(1)} %get-tuple-element.24), channel_id=1, source_target_pairs={{1,0},{2,1},{3,2},{4,3},{5,4},{6,5},{7,6},{8,7},{9,8},{10,9},{11,1... | collective-permute-start | bytes 32264 | tf_op jit(solution)/shard_map/ppermute | solution.py:27
  170.6 14.2 %collective-permute-start.2 = (f32[5,2,64,1]{3,2,1,0:T(8,128)S(1)}, f32[5,2,64,1]{3,2,1,0:T(8,128)S(1)}, u32[]{:S(2)}, u32[]{:S(2)}) collective-permute-start(f32[5,2,64,1]{3,2,1,0:T(8,128)S(1)} %get-tuple-element.21), channel_id=1, source_target_pairs={{0,1},{1,2},{2,3},{3,4},{4,5},{5,6},{6,7},{7,8},{8,9},{9,10},{10,1... | collective-permute-start | bytes 7688 | tf_op jit(solution)/shard_map/ppermute | solution.py:26
  173.8 14.9 %collective-permute-start.3 = (f32[5,2,64,1]{3,2,1,0:T(8,128)S(1)}, f32[5,2,64,1]{3,2,1,0:T(8,128)S(1)}, u32[]{:S(2)}, u32[]{:S(2)}) collective-permute-start(f32[5,2,64,1]{3,2,1,0:T(8,128)S(1)} %get-tuple-element.22), channel_id=1, source_target_pairs={{1,0},{2,1},{3,2},{4,3},{5,4},{6,5},{7,6},{8,7},{9,8},{10,9},{11,1... | collective-permute-start | bytes 7688 | tf_op jit(solution)/shard_map/ppermute | solution.py:27
  217.6 5.5 %copy-start.7 = (f32[32]{0:T(128)S(1)}, f32[32]{0:T(128)}, u32[]{:S(2)}) copy-start(f32[32]{0:T(128)} %param.13) | copy-start | bytes 388
  233.3 3.3 %copy-start.2 = (f32[32,2,64,256]{3,0,2,1:T(8,128)}, f32[32,2,64,256]{3,0,2,1:T(8,128)S(1)}, u32[]{:S(2)}) copy-start(f32[32,2,64,256]{3,0,2,1:T(8,128)S(1)} %maximum_bitcast_fusion) | copy-start | bytes 12582916
  233.3 8.4 %copy-start.6 = (f32[2,32,3,3]{1,0,3,2:T(2,128)S(1)}, f32[2,32,3,3]{1,0,3,2:T(2,128)}, u32[]{:S(2)}) copy-start(f32[2,32,3,3]{1,0,3,2:T(2,128)} %param.14) | copy-start | bytes 6916
  236.6 9.6 %copy-start.5 = (f32[32,2,64,1]{3,0,2,1:T(8,128)S(1)}, f32[32,2,64,1]{3,0,2,1:T(8,128)}, u32[]{:S(2)}) copy-start(f32[32,2,64,1]{3,0,2,1:T(8,128)} %get-tuple-element.12) | copy-start | bytes 49156
  239.4 14.0 %collective-permute-start.4 = (f32[32,2,64,1]{2,0,3,1:T(8,128)S(1)}, f32[32,2,64,1]{2,0,3,1:T(8,128)S(1)}, u32[]{:S(2)}, u32[]{:S(2)}) collective-permute-start(f32[32,2,64,1]{2,0,3,1:T(8,128)S(1)} %copy.95), channel_id=1, source_target_pairs={{0,1},{1,2},{2,3},{3,4},{4,5},{5,6},{6,7},{7,8},{8,9},{9,10},{10,1... | collective-permute-start | bytes 49160 | tf_op jit(solution)/shard_map/ppermute | solution.py:26
  247.3 12.8 %collective-permute-start.5 = (f32[32,2,64,1]{2,0,3,1:T(8,128)S(1)}, f32[32,2,64,1]{2,0,3,1:T(8,128)S(1)}, u32[]{:S(2)}, u32[]{:S(2)}) collective-permute-start(f32[32,2,64,1]{2,0,3,1:T(8,128)S(1)} %copy.96), channel_id=1, source_target_pairs={{1,0},{2,1},{3,2},{4,3},{5,4},{6,5},{7,6},{8,7},{9,8},{10,9},{11,1... | collective-permute-start | bytes 49160 | tf_op jit(solution)/shard_map/ppermute | solution.py:27
  275.6 5.5 %copy-start.8 = (f32[2]{0:T(128)S(1)}, f32[2]{0:T(128)}, u32[]{:S(2)}) copy-start(f32[2]{0:T(128)} %param.15) | copy-start | bytes 28
  278.3 5.3 %copy-start.3 = (f32[32,2,64,256]{3,0,2,1:T(8,128)S(1)}, f32[32,2,64,256]{3,0,2,1:T(8,128)}, u32[]{:S(2)}) copy-start(f32[32,2,64,256]{3,0,2,1:T(8,128)} %copy-done.2) | copy-start | bytes 12582916
  278.3 5.3 %copy-start.4 = (f32[32,2,64,1]{3,0,2,1:T(8,128)S(1)}, f32[32,2,64,1]{3,0,2,1:T(8,128)}, u32[]{:S(2)}) copy-start(f32[32,2,64,1]{3,0,2,1:T(8,128)} %copy.98) | copy-start | bytes 49156
  281.2 6.5 %copy-start.1 = (s32[32,1,64]{2,1,0:T(1,128)S(1)}, s32[32,1,64]{2,1,0:T(1,128)}, u32[]{:S(2)}) copy-start(s32[32,1,64]{2,1,0:T(1,128)} %param.9) | copy-start | bytes 24580
Sparse Core Ops, SparseCore 0:
  25.1 131.4 all-reduce.5
where the time goes:
time: 299 us; the launch traced here: 295 us
  waiting for transfers between devices  146 us (49%)
  matrix products  75.8 us (25%)
  starting transfers between devices  32 us (11%)
  local copies, waits for them, and re-layouts  16.7 us (6%)
  between operations  14.8 us (5%)
  other arithmetic  9.08 us (3%)
    psum x1, waiting for transfers between devices, from_root(): return lax.psum(jnp.where(mine, shard, jnp.zeros_like(shard)), axis)  131 us
    dot_general x18, matrix products, conv_taps(): jnp.einsum('oi,inpw->onpw', weights[:, :, tap_a, tap_b], bordered_patch[:...  74.5 us
    ppermute x3, starting transfers between devices, extended(): after = lax.ppermute(first, axis, down)  15.9 us
    ppermute x3, starting transfers between devices, extended(): before = lax.ppermute(last, axis, up)  8.91 us
    all_to_all x1, waiting for transfers between devices, local(): lax.all_to_all(slave_complex_pixels, 'date', split_axis=0, concat_axis=2,...  7.41 us
    all_to_all x1, starting transfers between devices, local(): lax.all_to_all(slave_complex_pixels, 'date', split_axis=0, concat_axis=2,...  7.17 us
    slice x3, local copies, waits for them, and re-layouts, extended(): last = lax.slice_in_dim(shard, length - width, length, axis=dim)  6.1 us
  transfers between devices with their start and end apart: 8, of which 5 were waited for; matrix products, arithmetic and copies ran while one was open for 6% of the time, Pallas kernels for 0%

commit v1 on v0

v1 whole, which is shorter than its diff:
```python
import jax
import jax.numpy as jnp
from jax import lax
from jax.experimental import pallas as pl
from jax.experimental.pallas import tpu as pltpu
from jax.sharding import PartitionSpec as P

BOX_AZ = 7
BOX_RG = 28
EPSILON = 1e-06
ROWS = 64
COLS = 256
BANDS = 16
EDGE = 16
BLOCKS = 8
TAPS = 240
F32 = jnp.float32
BF16 = jnp.bfloat16


def iota(shape, dim):
    return lax.broadcasted_iota(jnp.int32, shape, dim)


def halves(value):
    high = value.astype(BF16)
    return high, (value - high.astype(F32)).astype(BF16)


def matmul(left, right):
    return jnp.dot(left, right, preferred_element_type=F32)


def spread_kernel(first_ref, second_ref, first_out, second_out):
    row, col = iota((256, TAPS), 0), iota((256, TAPS), 1)
    tap = col % 16 - row % 8 - 3
    widen = (iota((256, 32), 0) // 8 == iota((256, 32), 1)).astype(BF16)
    source, target = iota((48, TAPS), 0), iota((48, TAPS), 1)
    base = (target % 80) // 16 * 9 + target // 80
    for part, piece in enumerate(halves(first_ref[...])):
        tall = matmul(widen, piece).astype(BF16)
        offset = ((source == 45) & (target == 0)).astype(BF16)
        spread = matmul(tall, offset)
        for a in range(3):
            chosen = (source == base + 3 * a).astype(BF16)
            spread = jnp.where(tap == a, matmul(tall, chosen), spread)
        first_out[256 * part : 256 * part + 256, :] = spread.astype(BF16)
    row, col = iota((64, 256), 0), iota((64, 256), 1)
    out_row = jnp.where(row < 48, row % 8, jnp.where(row < 54, -1, 8))
    tap = col % 8 - out_row + 1
    to_row, from_row = iota((64, 24), 0), iota((64, 24), 1)
    group = jnp.where(to_row < 48, to_row // 8, (to_row - 48) % 6)
    real = to_row < 60
    widen = (iota((32, 256), 1) // 8 == iota((32, 256), 0)).astype(BF16)
    for part, piece in enumerate(halves(second_ref[...])):
        wide = matmul(piece, widen).astype(BF16)
        spread = jnp.zeros((64, 256), F32)
        for a in range(3):
            chosen = (real & (from_row == group + 6 * a)).astype(BF16)
            spread = jnp.where(tap == a, matmul(chosen, wide), spread)
        second_out[64 * part : 64 * part + 64, :] = spread.astype(BF16)


def pick_kernel(chosen_ref, bands_ref, window_ref, first_ref, last_ref):
    lane = iota((ROWS, 128), 1)
    first = jnp.zeros((ROWS, 128), F32)
    last = jnp.zeros((ROWS, 128), F32)
    for slot in range(3):
        for part in range(2):
            k = 2 * slot + part
            rows = bands_ref[:, slot, part].astype(F32).reshape(8 * BANDS, COLS).astype(BF16)
            picked = matmul(chosen_ref[slot], rows)
            window_ref[slot, part] = picked.astype(BF16)
            here = (lane >= EDGE * k) & (lane < EDGE * (k + 1))
            left = picked[:, :128]
            right = pltpu.roll(picked[:, 128:], EDGE * (k + 1), 1)
            if k:
                left = pltpu.roll(left, EDGE * k, 1)
            first = jnp.where(here, left, first)
            last = jnp.where(here, right, last)
    first_ref[...] = first.astype(BF16)
    last_ref[...] = last.astype(BF16)


def products(re, im):
    ref_re, ref_im = re[2], im[2]
    pow_ref = ref_re * ref_re + ref_im * ref_im
    pow_sec = [re[d] * re[d] + im[d] * im[d] for d in range(2)]
    cross_re = [ref_re * re[d] + ref_im * im[d] for d in range(2)]
    cross_im = [ref_im * re[d] - ref_re * im[d] for d in range(2)]
    both = [jnp.sqrt(pow_ref * pow_sec[d]) for d in range(2)]
    return pow_ref, pow_sec, cross_re, cross_im, both


def sum_rows(summed, near_ref):
    high, low = halves(summed)
    return matmul(near_ref[...], jnp.concatenate([high, low], axis=0))


def features(boxed, log_ref, inside):
    inverse = 1.0 / (jnp.sqrt(boxed[0] * boxed[1]) + EPSILON)
    mean_log = jnp.log(boxed[0] / (BOX_AZ * BOX_RG) + EPSILON)
    return [
        boxed[2] * inverse,
        boxed[3] * inverse,
        boxed[4] * inverse,
        jnp.log(boxed[1] + EPSILON) - log_ref,
        jnp.where(inside, mean_log, 0.0),
    ]


def window_rows(width):
    row = iota((16 * BLOCKS, width), 0)
    frame_row = row // 16 * 8 - 4 + row % 16
    return (frame_row >= 0) & (frame_row < ROWS), row % 16 == 0


def store_taps(taken, first_row, high_ref, low_ref):
    width = taken[0].shape[1]
    for i, field in enumerate(taken):
        for b in range(3):
            moved = field if b == 1 else pltpu.roll(field, (1, 0, width - 1)[b], 1)
            if i == 0 and b == 0:
                moved = jnp.where(first_row, 1.0, moved)
            high, low = halves(moved)
            for j in range(BLOCKS):
                at = b * 80 + i * 16
                high_ref[j, at : at + 16, :] = high[16 * j : 16 * j + 16]
                low_ref[j, at : at + 16, :] = low[16 * j : 16 * j + 16]


def head_block(high, low, first_ref, second_ref, inside):
    doubled = matmul(first_ref[...], high)
    hidden = doubled[:256] + doubled[256:] + matmul(first_ref[:256, :], low)
    hidden = jnp.maximum(hidden, 0.0)
    if inside is not None:
        hidden = jnp.where(inside, hidden, 0.0)
    high, low = halves(hidden)
    doubled = matmul(second_ref[...], high)
    return doubled[:64] + doubled[64:] + matmul(second_ref[:64, :], low)


def joined(parts, j, group):
    width = parts[j].shape[1]
    row = iota((8, width), 0)
    value = parts[j][8 * group : 8 * group + 8]
    if j:
        below = parts[j - 1][54 + group : 55 + group]
        value = value + jnp.where(row == 0, below, 0.0)
    if j + 1 < BLOCKS:
        above = parts[j + 1][48 + group : 49 + group]
        value = value + jnp.where(row == 7, above, 0.0)
    return value


def class_rows(parts, j, o, shift_ref):
    width = parts[j].shape[1]
    before = pltpu.roll(joined(parts, j, o), 1, 1)
    after = pltpu.roll(joined(parts, j, 4 + o), width - 1, 1)
    return before + joined(parts, j, 2 + o) + after + shift_ref[o]


def middle_kernel(shift_ref, window_ref, near_ref, first_ref, second_ref, out_ref, high_ref, low_ref):
    re = [window_ref[s, 0].astype(F32) for s in range(3)]
    im = [window_ref[s, 1].astype(F32) for s in range(3)]
    pow_ref, pow_sec, cross_re, cross_im, both = products(re, im)
    gap = iota((COLS, COLS), 0) - iota((COLS, COLS), 1) + BOX_RG // 2
    band = ((gap >= 0) & (gap < BOX_RG)).astype(BF16)
    band = jnp.concatenate([band, band], axis=0)
    inside, first_row = window_rows(COLS)

    def boxed(plane):
        summed = matmul(jnp.concatenate(halves(plane), axis=1), band)
        return sum_rows(summed, near_ref)

    box_ref = boxed(pow_ref)
    log_ref = jnp.log(box_ref + EPSILON)
    for d in range(2):
        sums = [box_ref] + [boxed(p[d]) for p in (pow_sec, cross_re, cross_im, both)]
        store_taps(features(sums, log_ref, inside), first_row, high_ref.at[d], low_ref.at[d])
    for d in range(2):
        parts = [
            head_block(high_ref[d, j], low_ref[d, j], first_ref, second_ref, None) for j in range(BLOCKS)
        ]
        for j in range(BLOCKS):
            for o in range(2):
                out_ref[d, o, 8 * j : 8 * j + 8, :] = class_rows(parts, j, o, shift_ref)


def edge_kernel(
    place_ref, shift_ref, window_ref, before_ref, after_ref, near_ref, first_ref, second_ref, done_ref,
    out_ref, high_ref, low_ref,
):
    lane = iota((ROWS, 128), 1)
    before, after = before_ref[...].astype(F32), after_ref[...].astype(F32)

    def pixels(slot, part):
        k = 2 * slot + part
        value = window_ref[slot, part].astype(F32)
        own_first = pltpu.roll(value[:, :128], EDGE, 1)
        own_last = pltpu.roll(value[:, 128:], 96, 1)
        left = pltpu.roll(before, 128 - EDGE * k, 1) if k else before
        right = pltpu.roll(after, (96 - EDGE * k) % 128, 1) if k != 6 else after
        tile = jnp.where(lane < EDGE, left, own_first)
        tile = jnp.where(lane < 64, tile, own_last)
        tile = jnp.where(lane < 96, tile, right)
        return jnp.where(lane < 112, tile, 0.0)

    re = [pixels(s, 0) for s in range(3)]
    im = [pixels(s, 1) for s in range(3)]
    pow_ref, pow_sec, cross_re, cross_im, both = products(re, im)
    source, target = iota((128, 128), 0), iota((128, 128), 1)
    from_col = jnp.where(source < 64, source - 16, source + 160)
    side = target % 64 // 32
    to_col = target % 32 + jnp.where(side == 0, -4, 232)
    gap = from_col - to_col + BOX_RG // 2
    near = (gap >= 0) & (gap < BOX_RG) & (source // 64 == side)
    bands = [(near & (target // 64 == d)).astype(BF16) for d in range(2)]
    band = jnp.concatenate([bands[0], bands[0], bands[1], bands[1]], axis=0)

    def boxed(planes):
        pieces = halves(planes[0]) + halves(planes[1])
        return sum_rows(matmul(jnp.concatenate(pieces, axis=1), band), near_ref)

    inside, first_row = window_rows(128)
    place = place_ref[0]

    def in_frame(rows):
        spot = iota((rows, 128), 1)
        column = spot % 32 + jnp.where(spot % 64 < 32, -4, 232)
        low = jnp.where(place == 0, 0, -128)
        high = jnp.where(place == place_ref[1] - 1, COLS, 2 * COLS)
        return (column >= low) & (column < high)

    valid = in_frame(16 * BLOCKS)
    sums = [boxed([pow_ref, pow_ref])] + [boxed(p) for p in (pow_sec, cross_re, cross_im, both)]
    taken = features(sums, jnp.log(sums[0] + EPSILON), inside)
    store_taps([jnp.where(valid, f, 0.0) for f in taken], first_row, high_ref, low_ref)
    kept = in_frame(256)
    parts = [head_block(high_ref[j], low_ref[j], first_ref, second_ref, kept) for j in range(BLOCKS)]
    spot = iota((8, 128), 1)
    for j in range(BLOCKS):
        for o in range(2):
            value = class_rows(parts, j, o, shift_ref)
            at = slice(8 * j, 8 * j + 8)
            for d in range(2):
                left = pltpu.roll(value, 128 - 64 * d - 4, 1)
                right = pltpu.roll(value, (112 - 64 * d - 40) % 128, 1)
                out_ref[d, o, at, :128] = jnp.where(spot < EDGE, left, done_ref[d, o, at, :128])
                out_ref[d, o, at, 128:] = jnp.where(spot >= 112, right, done_ref[d, o, at, 128:])


def vmem():
    return pl.BlockSpec(memory_space=pltpu.VMEM)


def smem():
    return pl.BlockSpec(memory_space=pltpu.SMEM)


def local(
    slave_complex_pixels,
    along_track_line_groups,
    master_epoch_position,
    sweep_identifier,
    initial_filter_kernel,
    initial_filter_shift,
    latter_filter_kernel,
    latter_filter_shift,
):
    date_index = lax.axis_index("date")
    rng_count = lax.axis_size("rng")
    chosen = master_epoch_position[0]
    own = slave_complex_pixels.reshape(BANDS, 2, 2, 8, COLS)
    master = lax.dynamic_slice_in_dim(slave_complex_pixels, chosen, 1, 0)[None]
    sent = jnp.concatenate([own, jnp.broadcast_to(master, (BANDS, 1, 2, 8, COLS))], axis=1)
    bands = lax.all_to_all(sent, "date", split_axis=0, concat_axis=0, tiled=True)

    lists = along_track_line_groups[:, 0, :]
    mine = lax.dynamic_slice_in_dim(lists, date_index * 2, 2, 0)
    lists = jnp.concatenate([mine, lax.dynamic_slice_in_dim(lists, chosen, 1, 0)], axis=0)
    row_of = lax.broadcasted_iota(jnp.int32, (3, ROWS, 8 * BANDS), 2)
    picks = (lists[:, :, None] == row_of).astype(BF16)

    window = jnp.arange(16 * BLOCKS)
    frame_row = window // 16 * 8 - 4 + window % 16
    row_id = jnp.arange(ROWS)
    burst = sweep_identifier.astype(jnp.int32)
    target_burst = jnp.where(window // 16 * 8 - 4 + window % 16 < 0, -1, 0) + jnp.sum(
        jnp.where(frame_row[:, None] == row_id[None, :], burst[None, :], 0), axis=1
    )
    near = (
        (jnp.abs(row_id[None, :] - frame_row[:, None]) <= BOX_AZ // 2)
        & (burst[None, :] == target_burst[:, None])
        & (frame_row >= 0)[:, None]
        & (frame_row < ROWS)[:, None]
    ).astype(BF16)
    near = jnp.concatenate([near, near], axis=1)

    first = jnp.concatenate(
        [
            initial_filter_kernel.reshape(32, 45),
            initial_filter_shift[:, None],
            jnp.zeros((32, 2), F32),
        ],
        axis=1,
    )
    second = jnp.pad(jnp.transpose(latter_filter_kernel, (2, 3, 0, 1)).reshape(18, 32), ((0, 6), (0, 0)))
    first_spread, second_spread = pl.pallas_call(
        spread_kernel,
        out_shape=(
            jax.ShapeDtypeStruct((512, TAPS), BF16),
            jax.ShapeDtypeStruct((128, 256), BF16),
        ),
        in_specs=[vmem()] * 2,
        out_specs=(vmem(), vmem()),
        cost_estimate=pl.CostEstimate(flops=10**7, bytes_accessed=10**6, transcendentals=0),
    )(first, second)

    pixels, first_edge, last_edge = pl.pallas_call(
        pick_kernel,
        out_shape=(
            jax.ShapeDtypeStruct((3, 2, ROWS, COLS), BF16),
            jax.ShapeDtypeStruct((ROWS, 128), BF16),
            jax.ShapeDtypeStruct((ROWS, 128), BF16),
        ),
        in_specs=[vmem()] * 2,
        out_specs=(vmem(),) * 3,
    )(picks, bands)

    up = [(i, i + 1) for i in range(rng_count - 1)]
    down = [(i + 1, i) for i in range(rng_count - 1)]
    before = lax.ppermute(last_edge, "rng", up)
    after = lax.ppermute(first_edge, "rng", down)

    middle = pl.pallas_call(
        middle_kernel,
        out_shape=jax.ShapeDtypeStruct((2, 2, ROWS, COLS), F32),
        in_specs=[smem()] + [vmem()] * 4,
        out_specs=vmem(),
        scratch_shapes=[
            pltpu.VMEM((2, BLOCKS, TAPS, COLS), BF16),
            pltpu.VMEM((2, BLOCKS, TAPS, COLS), BF16),
        ],
        cost_estimate=pl.CostEstimate(flops=4 * 10**9, bytes_accessed=10**7, transcendentals=10**5),
    )(latter_filter_shift, pixels, near, first_spread, second_spread)

    place = jnp.stack([lax.axis_index("rng"), jnp.int32(rng_count)]).astype(jnp.int32)
    return pl.pallas_call(
        edge_kernel,
        out_shape=jax.ShapeDtypeStruct((2, 2, ROWS, COLS), F32),
        in_specs=[smem()] * 2 + [vmem()] * 7,
        out_specs=vmem(),
        scratch_shapes=[
            pltpu.VMEM((BLOCKS, TAPS, 128), BF16),
            pltpu.VMEM((BLOCKS, TAPS, 128), BF16),
        ],
        input_output_aliases={8: 0},
    )(place, latter_filter_shift, pixels, before, after, near, first_spread, second_spread, middle)


def solution(mesh):
    placed = (P(None, None, "date", "rng"), P(None, "rng", None), P(), P(), P(), P(), P(), P())
    return jax.shard_map(
        local, mesh=mesh, in_specs=placed, out_specs=P("date", None, None, "rng"), check_vma=False
    )
```

time: 299 us -> 49.6 us (0.17); the launches traced: 295 us -> 49.1 us
  waiting for transfers between devices: 146 us -> 3.6 us
  matrix products: 75.8 us -> 0 us
  Pallas kernels: 0 us -> 20.7 us
  starting transfers between devices: 32 us -> 15.1 us
  between operations: 14.8 us -> 0.81 us
  local copies, waits for them, and re-layouts: 16.7 us -> 4.21 us
  other arithmetic: 9.08 us -> 4.77 us
    psum x1 -> x0, waiting for transfers between devices: 131 us -> none  [from_root(): return lax.psum(jnp.where(mine, shard, jnp.zeros_like(shard)), axis)]
    dot_general x20 -> x0, matrix products: 75.8 us -> none  [the longest x18 74.5 us: conv_taps(): jnp.einsum('oi,inpw->onpw', weights[:, :, tap_a, tap_b], bordered_patch[:...]
    pallas_call x0 -> x4, Pallas kernels: none -> 20.7 us  [the longest x1 10.1 us: local(): pl.pallas_call(middle_kernel, out_shape=jax.ShapeDtypeStruct((2, 2, ROWS,...]
    ppermute x6 -> x2, starting transfers between devices: 24.8 us -> 7.94 us  [the longest x1 5.37 us: local(): after = lax.ppermute(first_edge, 'rng', down)]
    slice x6 -> x0, local copies, waits for them, and re-layouts: 8.92 us -> none  [the longest x3 6.1 us: extended(): last = lax.slice_in_dim(shard, length - width, length, axis=dim)]
    ppermute x6 -> x2, waiting for transfers between devices: 7.45 us -> 0.01 us  [the longest x1 0.01 us: local(): before = lax.ppermute(last_edge, 'rng', up)]
    ppermute x2 -> x0, local copies, waits for them, and re-layouts: 4.79 us -> none  [the longest x1 2.93 us: extended(): after = lax.ppermute(first, axis, down)]
    all_to_all x1, waiting for transfers between devices: 7.41 us -> 3.59 us  [local(): lax.all_to_all(sent, 'date', split_axis=0, concat_axis=0, tiled=True)]
  transfers between devices with their start and end apart: 8 -> 3, of which waited for: 5 -> 1; matrix products, arithmetic and copies ran while one was open for 6% -> 8% of each run, Pallas kernels for 0% -> 25%
where the time goes in v1:
time: 49.6 us; the launch traced here: 49.1 us
  Pallas kernels  20.7 us (42%)
  starting transfers between devices  15.1 us (30%)
  other arithmetic  4.77 us (10%)
  local copies, waits for them, and re-layouts  4.21 us (8%)
  waiting for transfers between devices  3.6 us (7%)
  between operations  0.81 us (2%)
    pallas_call x1, Pallas kernels, local(): pl.pallas_call(middle_kernel, out_shape=jax.ShapeDtypeStruct((2, 2, ROWS,...  10.1 us
    all_to_all x1, starting transfers between devices, local(): lax.all_to_all(sent, 'date', split_axis=0, concat_axis=0, tiled=True)  7.17 us
    pallas_call x1, Pallas kernels, local(): pl.pallas_call(edge_kernel, out_shape=jax.ShapeDtypeStruct((2, 2, ROWS, C...  6.37 us
    ppermute x1, starting transfers between devices, local(): after = lax.ppermute(first_edge, 'rng', down)  5.37 us
    all_to_all x1, waiting for transfers between devices, local(): lax.all_to_all(sent, 'date', split_axis=0, concat_axis=0, tiled=True)  3.59 us
    unnamed x16, local copies, waits for them, and re-layouts  2.61 us
    ppermute x1, starting transfers between devices, local(): before = lax.ppermute(last_edge, 'rng', up)  2.57 us
    pallas_call x1, Pallas kernels, local(): pl.pallas_call(spread_kernel, out_shape=(jax.ShapeDtypeStruct((512, TAPS)...  2.29 us
  transfers between devices with their start and end apart: 3, of which 1 were waited for; matrix products, arithmetic and copies ran while one was open for 8% of the time, Pallas kernels for 25%

profile of v1, /device:TPU:128, one launch (start us, length us, event | category | flops | bytes accessed | tf_op | source)
XLA Modules:
  0.0 49.1 jit_solution(8789256568040291248)
XLA Ops:
  0.0 0.0 copy-start
  0.7 0.7 %dynamic-slice_bitcast_fusion = bf16[2,8,256]{2,1,0:T(8,128)(2,1)S(1)} fusion(bf16[32,2,8,256]{3,2,1,0:T(8,128)(2,1)} %param.8, s32[]{:T(128)S(6)} %select_n.77), kind=kLoop, calls=%fused_computation.11 | loop fusion | bytes 16388 | tf_op jit(solution)/shard_map/broadcast_in_dim | solution.py:276
  1.4 1.7 %pad_maximum_fusion = bf16[16,3,2,8,256]{4,3,2,1,0:T(8,128)(2,1)} fusion(bf16[16,1,2,8,256]{4,3,2,1,0:T(8,128)(2,1)S(1)} %broadcast_in_dim.23, bf16[16,2,2,8,256]{4,3,2,1,0:T(8,128)(2,1)} %bitcast.15), kind=kLoop, calls=%fused_computation | loop fusion | flops 196608 | bytes 786432 | tf_op jit(solution)/shard_map/concatenate | solution.py:276
  3.1 0.0 copy-start.7
  3.1 7.2 %all-to-all-start = ((bf16[16,3,2,8,256]{4,3,2,1,0:T(8,128)(2,1)}), bf16[16,3,2,8,256]{4,3,2,1,0:T(8,128)(2,1)S(1)}, u32[]{:S(2)}, u32[]{:S(2)}) async-start(bf16[16,3,2,8,256]{4,3,2,1,0:T(8,128)(2,1)} %pad_maximum_fusion), calls=%async_computation | async-start | bytes 786432 | tf_op jit(solution)/shard_map/all_to_all | solution.py:277
  10.3 0.0 copy-start.2
  10.3 0.0 copy-done.7
  10.4 0.2 select_reduce_fusion
  10.5 0.0 copy-done
  10.6 0.0 copy-start.6
  10.6 0.6 %copy-done.6 = f32[32]{0:T(128)S(1)} copy-done((f32[32]{0:T(128)S(1)}, f32[32]{0:T(128)}, u32[]{:S(2)}) %copy-start.6) | copy-done | bytes 152
  11.2 0.1 copy.13
  11.3 0.0 copy-done.2
  11.4 0.1 copy.12
  11.5 0.1 pad.7.clone
  11.5 0.1 fusion.3
  11.7 0.0 copy-start.5
  11.7 0.7 %maximum_maximum_fusion.first_ref = f32[32,48]{1,0:T(8,128)} fusion(f32[32,1]{1,0:T(8,128)S(1)} %copy.13, f32[32,45]{1,0:T(8,128)S(1)} %copy.12, f32[48]{0:T(128)S(1)} %pad.7.clone), kind=kLoop, calls=%fused_computation.10 | loop fusion | flops 3072 | bytes 12224 | tf_op jit(solution)/shard_map/concatenate | solution.py:300
  12.4 0.6 %pad_add_fusion.1.place_ref = s32[2]{0:T(128)} fusion(s32[1]{0:T(128)} %constant.57.clone.1, s32[1]{0:T(128)} %bitcast), kind=kLoop, calls=%fused_computation.26 | loop fusion | flops 2 | bytes 16 | tf_op jit(solution)/shard_map/stack | solution.py:348
  13.0 0.0 copy-done.5
  13.0 0.6 %pad.4.second_ref = f32[24,32]{1,0:T(8,128)} pad(f32[18,32]{1,0:T(8,128)S(1)} %reshape.54, f32[]{:T(128)} %constant.71.clone.1), padding=0_6x0_0 | pad | bytes 5380 | tf_op jit(solution)/shard_map/jit(_pad)/pad | solution.py:308
  13.6 2.3 %shard_map.83 = (bf16[512,240]{1,0:T(8,128)(2,1)}, bf16[128,256]{1,0:T(8,128)(2,1)}) custom-call(f32[32,48]{1,0:T(8,128)} %maximum_maximum_fusion.first_ref, f32[24,32]{1,0:T(8,128)} %pad.4.second_ref), custom_call_target="tpu_custom_call" | custom-call | flops 10000000 | bytes 1000000 | tf_op jit(solution)/shard_map/pallas_call | solution.py:309
  15.9 0.7 %add_convert_fusion.near_ref = bf16[128,128]{1,0:T(8,128)(2,1)} fusion(pred[128,64]{1,0:T(8,128)(4,1)S(1)} %fusion.3), kind=kLoop, calls=%fused_computation.9 | loop fusion | flops 32768 | bytes 40960 | tf_op jit(solution)/shard_map/concatenate | solution.py:298
  16.6 0.7 %fusion.chosen_ref = bf16[3,64,128]{2,1,0:T(8,128)(2,1)} fusion(s32[3,64]{1,0:T(4,128)S(1)} %pad_add_fusion), kind=kLoop, calls=%fused_computation.2 | loop fusion | flops 49152 | bytes 49920 | tf_op jit(solution)/shard_map/convert_element_type | solution.py:283
  17.3 3.6 %all-to-all-done.bands_ref = bf16[16,3,2,8,256]{4,3,2,1,0:T(8,128)(2,1)S(1)} async-done(((bf16[16,3,2,8,256]{4,3,2,1,0:T(8,128)(2,1)}), bf16[16,3,2,8,256]{4,3,2,1,0:T(8,128)(2,1)S(1)}, u32[]{:S(2)}, u32[]{:S(2)}) %all-to-all-start) | async-done | bytes 393248 | tf_op jit(solution)/shard_map/all_to_all | solution.py:277
  20.9 0.0 copy-start.1
  20.9 0.7 %copy-done.1 = bf16[16,3,2,8,256]{4,3,2,1,0:T(8,128)(2,1)} copy-done((bf16[16,3,2,8,256]{4,3,2,1,0:T(8,128)(2,1)}, bf16[16,3,2,8,256]{4,3,2,1,0:T(8,128)(2,1)S(1)}, u32[]{:S(2)}) %copy-start.1) | copy-done | bytes 393240
  21.6 1.9 %shard_map.82 = (bf16[3,2,64,256]{3,2,1,0:T(8,128)(2,1)}, bf16[64,128]{1,0:T(8,128)(2,1)}, bf16[64,128]{1,0:T(8,128)(2,1)}) custom-call(bf16[3,64,128]{2,1,0:T(8,128)(2,1)} %fusion.chosen_ref, bf16[16,3,2,8,256]{4,3,2,1,0:T(8,128)(2,1)} %copy-done.1), custom_call_target="tpu_custom_call" | custom-call | tf_op jit(solution)/shard_map/pallas_call | solution.py:320
  23.5 2.6 %collective-permute-start = (bf16[64,128]{1,0:T(8,128)(2,1)}, bf16[64,128]{1,0:T(8,128)(2,1)S(1)}, u32[]{:S(2)}, u32[]{:S(2)}) collective-permute-start(bf16[64,128]{1,0:T(8,128)(2,1)} %get-tuple-element.11), channel_id=1, source_target_pairs={{0,1},{1,2},{2,3},{3,4},{4,5},{5,6},{6,7},{7,8},{8,9},{9,10},{10,1... | collective-permute-start | bytes 49160 | tf_op jit(solution)/shard_map/ppermute | solution.py:333
  26.1 5.4 %collective-permute-start.1 = (bf16[64,128]{1,0:T(8,128)(2,1)}, bf16[64,128]{1,0:T(8,128)(2,1)S(1)}, u32[]{:S(2)}, u32[]{:S(2)}) collective-permute-start(bf16[64,128]{1,0:T(8,128)(2,1)} %get-tuple-element.12), channel_id=1, source_target_pairs={{1,0},{2,1},{3,2},{4,3},{5,4},{6,5},{7,6},{8,7},{9,8},{10,9},{11,1... | collective-permute-start | bytes 49160 | tf_op jit(solution)/shard_map/ppermute | solution.py:334
  31.5 10.1 %shard_map.84.done_ref = f32[2,2,64,256]{3,2,1,0:T(8,128)} custom-call(f32[2]{0:T(128)} %shift_ref.3, bf16[3,2,64,256]{3,2,1,0:T(8,128)(2,1)} %get-tuple-element.10.window_ref, bf16[128,128]{1,0:T(8,128)(2,1)} %add_convert_fusion.near_ref, bf16[512,240]{1,0:T(8,128)(2,1)} %get-tuple-element.13.first_ref, bf16[128,256]{1,0:T(8,128)(2,1)} %get-tuple-element.14.second_ref), custom_call_target="tpu_custom_call" | custom-call | flops 4000000000 | bytes 10000000 | tf_op jit(solution)/shard_map/pallas_call | solution.py:336
  41.6 0.0 collective-permute-done.before_ref
  41.6 0.0 copy-start.3
  41.6 0.0 collective-permute-done.1.after_ref
  41.6 0.6 %copy-done.3 = bf16[64,128]{1,0:T(8,128)(2,1)} copy-done((bf16[64,128]{1,0:T(8,128)(2,1)}, bf16[64,128]{1,0:T(8,128)(2,1)S(1)}, u32[]{:S(2)}) %copy-start.3) | copy-done | bytes 16408
  42.2 0.0 copy-start.4
  42.2 0.6 %copy-done.4 = bf16[64,128]{1,0:T(8,128)(2,1)} copy-done((bf16[64,128]{1,0:T(8,128)(2,1)}, bf16[64,128]{1,0:T(8,128)(2,1)S(1)}, u32[]{:S(2)}) %copy-start.4) | copy-done | bytes 16408
  42.8 6.4 %shard_map.85 = f32[2,2,64,256]{3,2,1,0:T(8,128)} custom-call(s32[2]{0:T(128)} %pad_add_fusion.1.place_ref, f32[2]{0:T(128)} %shift_ref.3, bf16[3,2,64,256]{3,2,1,0:T(8,128)(2,1)} %get-tuple-element.10.window_ref, bf16[64,128]{1,0:T(8,128)(2,1)} %copy-done.3, bf16[64,128]{1,0:T(8,128)(2,1)} %copy-done.4, ...), custom_call_target="tpu_custom_call", output_to_operand_aliasing={{}: (8, {})} | custom-call | tf_op jit(solution)/shard_map/pallas_call | solution.py:349
  (10 shorter events, 0.1 us)
Async XLA Ops:
  0.0 10.5 %copy-start = (s32[32,1,64]{2,1,0:T(1,128)S(1)}, s32[32,1,64]{2,1,0:T(1,128)}, u32[]{:S(2)}) copy-start(s32[32,1,64]{2,1,0:T(1,128)} %param.9) | copy-start | bytes 24580
  3.1 7.2 %copy-start.7 = (s32[64]{0:T(128)S(1)}, s32[64]{0:T(128)}, u32[]{:S(2)}) copy-start(s32[64]{0:T(128)} %param.11) | copy-start | bytes 772
  3.1 17.8 %all-to-all-start = ((bf16[16,3,2,8,256]{4,3,2,1,0:T(8,128)(2,1)}), bf16[16,3,2,8,256]{4,3,2,1,0:T(8,128)(2,1)S(1)}, u32[]{:S(2)}, u32[]{:S(2)}) async-start(bf16[16,3,2,8,256]{4,3,2,1,0:T(8,128)(2,1)} %pad_maximum_fusion), calls=%async_computation | async-start | bytes 786432 | tf_op jit(solution)/shard_map/all_to_all | solution.py:277
  10.3 1.0 %copy-start.2 = (f32[32,5,3,3]{0,3,2,1:T(4,128)S(1)}, f32[32,5,3,3]{0,3,2,1:T(4,128)}, u32[]{:S(2)}) copy-start(f32[32,5,3,3]{0,3,2,1:T(4,128)} %param.12) | copy-start | bytes 17284
  10.6 0.7 %copy-start.6 = (f32[32]{0:T(128)S(1)}, f32[32]{0:T(128)}, u32[]{:S(2)}) copy-start(f32[32]{0:T(128)} %param.13) | copy-start | bytes 388
  11.7 1.3 %copy-start.5 = (f32[2,32,3,3]{1,0,3,2:T(2,128)S(1)}, f32[2,32,3,3]{1,0,3,2:T(2,128)}, u32[]{:S(2)}) copy-start(f32[2,32,3,3]{1,0,3,2:T(2,128)} %param.14) | copy-start | bytes 6916
  20.9 0.7 %copy-start.1 = (bf16[16,3,2,8,256]{4,3,2,1,0:T(8,128)(2,1)}, bf16[16,3,2,8,256]{4,3,2,1,0:T(8,128)(2,1)S(1)}, u32[]{:S(2)}) copy-start(bf16[16,3,2,8,256]{4,3,2,1,0:T(8,128)(2,1)S(1)} %all-to-all-done.bands_ref) | copy-start | bytes 1179652
  23.5 18.0 %collective-permute-start = (bf16[64,128]{1,0:T(8,128)(2,1)}, bf16[64,128]{1,0:T(8,128)(2,1)S(1)}, u32[]{:S(2)}, u32[]{:S(2)}) collective-permute-start(bf16[64,128]{1,0:T(8,128)(2,1)} %get-tuple-element.11), channel_id=1, source_target_pairs={{0,1},{1,2},{2,3},{3,4},{4,5},{5,6},{6,7},{7,8},{8,9},{9,10},{10,1... | collective-permute-start | bytes 49160 | tf_op jit(solution)/shard_map/ppermute | solution.py:333
  26.1 15.5 %collective-permute-start.1 = (bf16[64,128]{1,0:T(8,128)(2,1)}, bf16[64,128]{1,0:T(8,128)(2,1)S(1)}, u32[]{:S(2)}, u32[]{:S(2)}) collective-permute-start(bf16[64,128]{1,0:T(8,128)(2,1)} %get-tuple-element.12), channel_id=1, source_target_pairs={{1,0},{2,1},{3,2},{4,3},{5,4},{6,5},{7,6},{8,7},{9,8},{10,9},{11,1... | collective-permute-start | bytes 49160 | tf_op jit(solution)/shard_map/ppermute | solution.py:334
  41.6 0.6 %copy-start.3 = (bf16[64,128]{1,0:T(8,128)(2,1)}, bf16[64,128]{1,0:T(8,128)(2,1)S(1)}, u32[]{:S(2)}) copy-start(bf16[64,128]{1,0:T(8,128)(2,1)S(1)} %collective-permute-done.before_ref) | copy-start | bytes 49156
  42.2 0.6 %copy-start.4 = (bf16[64,128]{1,0:T(8,128)(2,1)}, bf16[64,128]{1,0:T(8,128)(2,1)S(1)}, u32[]{:S(2)}) copy-start(bf16[64,128]{1,0:T(8,128)(2,1)S(1)} %collective-permute-done.1.after_ref) | copy-start | bytes 49156

commit v2 on v1

v2 whole, which is shorter than its diff:
```python
import jax
import jax.numpy as jnp
from jax import lax
from jax.experimental import pallas as pl
from jax.experimental.pallas import tpu as pltpu
from jax.sharding import PartitionSpec as P

BOX_AZ = 7
BOX_RG = 28
EPSILON = 1e-06
ROWS = 64
COLS = 256
BANDS = 16
EDGE = 16
STEP = 6
BLOCKS = 11
WINDOWS = 12
HIDDEN = 32
WIDE = STEP * HIDDEN
F32 = jnp.float32
BF16 = jnp.bfloat16


def iota(shape, dim):
    return lax.broadcasted_iota(jnp.int32, shape, dim)


def halves(value):
    high = value.astype(BF16)
    return high, (value - high.astype(F32)).astype(BF16)


def matmul(left, right):
    return jnp.dot(left, right, preferred_element_type=F32)


def send_kernel(chosen_ref, own_ref, sent_ref):
    chosen = chosen_ref[0]
    sent_ref[:, :2] = own_ref[...]
    master = own_ref[chosen // 2, chosen % 2]
    for band in range(BANDS):
        sent_ref[band, 2] = master


def spread_kernel(first_ref, second_ref, shift_ref, first_out, second_out, shift_out):
    row, col = iota((WIDE, 128), 0), iota((WIDE, 128), 1)
    tap = col % 8 - row // HIDDEN
    widen = (iota((WIDE, HIDDEN), 0) % HIDDEN == iota((WIDE, HIDDEN), 1)).astype(BF16)
    source, target = iota((48, 128), 0), iota((48, 128), 1)
    piece = target // 8
    shift = jnp.where(piece < 6, piece // 2, jnp.where(piece < 12, piece // 2 - 3, piece - 12))
    feature = jnp.where(piece < 6, piece % 2, jnp.where(piece < 12, 2 + piece % 2, 4))
    base = feature * 9 + shift
    offset = ((source == 45) & (target == 120)).astype(BF16)
    taken = [((source == base + 3 * a) & (piece < 15)).astype(BF16) for a in range(3)]
    for part, half in enumerate(halves(first_ref[...])):
        tall = matmul(widen, half).astype(BF16)
        spread = jnp.zeros((WIDE, 128), F32)
        for a in range(3):
            spread = jnp.where(tap == a, matmul(tall, taken[a]), spread)
        at = slice(WIDE * part, WIDE * part + WIDE)
        first_out[at, :128] = (spread + matmul(tall, offset)).astype(BF16)
        first_out[at, 128:] = (spread if part == 0 else jnp.zeros_like(spread)).astype(BF16)
    row, col = iota((48, WIDE), 0), iota((48, WIDE), 1)
    tap = col // HIDDEN + 2 - row % 8
    widen = (iota((HIDDEN, WIDE), 1) % HIDDEN == iota((HIDDEN, WIDE), 0)).astype(BF16)
    group, source = iota((48, 24), 0) // 8, iota((48, 24), 1)
    for part, half in enumerate(halves(second_ref[...])):
        wide = matmul(half, widen).astype(BF16)
        spread = jnp.zeros((48, WIDE), F32)
        for a in range(3):
            chosen = (source == group + 6 * a).astype(BF16)
            spread = jnp.where(tap == a, matmul(chosen, wide), spread)
        second_out[48 * part : 48 * part + 48, :] = spread.astype(BF16)
    for o in range(2):
        shift_out[o] = jnp.full((8, 128), shift_ref[o], F32)


def pick_kernel(chosen_ref, bands_ref, window_ref, first_ref, last_ref):
    lane = iota((ROWS, 128), 1)
    first = jnp.zeros((ROWS, 128), F32)
    last = jnp.zeros((ROWS, 128), F32)
    for slot in range(3):
        for part in range(2):
            k = 2 * slot + part
            rows = bands_ref[:, slot, part].astype(F32).reshape(8 * BANDS, COLS).astype(BF16)
            picked = matmul(chosen_ref[slot], rows)
            window_ref[slot, part] = picked.astype(BF16)
            here = (lane >= EDGE * k) & (lane < EDGE * (k + 1))
            left = picked[:, :128]
            right = pltpu.roll(picked[:, 128:], EDGE * (k + 1), 1)
            if k:
                left = pltpu.roll(left, EDGE * k, 1)
            first = jnp.where(here, left, first)
            last = jnp.where(here, right, last)
    first_ref[...] = first.astype(BF16)
    last_ref[...] = last.astype(BF16)


def products(re, im):
    ref_re, ref_im = re[2], im[2]
    pow_ref = ref_re * ref_re + ref_im * ref_im
    planes = [pow_ref]
    for d in range(2):
        pow_sec = re[d] * re[d] + im[d] * im[d]
        planes += [
            pow_sec,
            ref_re * re[d] + ref_im * im[d],
            ref_im * re[d] - ref_re * im[d],
            jnp.sqrt(pow_ref * pow_sec),
        ]
    return planes


def sum_rows(summed, near_ref):
    return matmul(near_ref[...], jnp.concatenate(halves(summed), axis=0))


def mean_log(box_ref, inside):
    return jnp.where(inside, jnp.log(box_ref / (BOX_AZ * BOX_RG) + EPSILON), 0.0)


def features(box_ref, log_ref, boxed):
    inverse = 1.0 / (jnp.sqrt(box_ref * boxed[0]) + EPSILON)
    ratio = jnp.log(boxed[0] + EPSILON) - log_ref
    return boxed[1] * inverse, boxed[2] * inverse, boxed[3] * inverse, ratio


def window_rows(rows, base):
    row = iota(rows, 0)
    frame_row = row // 8 * STEP - 1 + row % 8 + base
    return (frame_row >= 0) & (frame_row < ROWS)


def sideways(value, b, span):
    if b == 1:
        return value
    width = value.shape[1]
    if span == width:
        return pltpu.roll(value, 1 if b == 0 else width - 1, 1)
    pieces = [sideways(value[:, at : at + span], b, span) for at in range(0, width, span)]
    return jnp.concatenate(pieces, axis=1)


def store_pieces(taps_ref, piece, upper, lower):
    for j in range(taps_ref.shape[0]):
        at = slice(8 * j, 8 * j + 8)
        high, low = halves(jnp.concatenate([upper[at], lower[at]], axis=0))
        taps_ref[j, 8 * piece : 8 * piece + 16, :] = high
        taps_ref[j, 128 + 8 * piece : 144 + 8 * piece, :] = low


def store_taps(taken, taps_ref, span):
    for pair in range(2):
        for b in range(3):
            upper, lower = [sideways(taken[2 * pair + k], b, span) for k in range(2)]
            store_pieces(taps_ref, 6 * pair + 2 * b, upper, lower)


def store_shared(shared, taps_refs, span):
    moved = [sideways(shared, b, span) for b in range(3)]
    one = jnp.where(iota(shared.shape, 0) % 8 == 0, 1.0, 0.0)
    for taps_ref in taps_refs:
        store_pieces(taps_ref, 12, moved[0], moved[1])
        store_pieces(taps_ref, 14, moved[2], one)


def head_block(taps, first_ref, second_ref, keep):
    doubled = matmul(first_ref[...], taps)
    hidden = jnp.maximum(doubled[:WIDE] + doubled[WIDE:], 0.0)
    high, low = halves(keep(hidden))
    doubled = matmul(second_ref[...], high)
    return doubled[:48] + doubled[48:] + matmul(second_ref[:48, :], low)


def class_window(parts, o, span):
    groups = [parts[16 * b + 8 * o : 16 * b + 8 * o + 8] for b in range(3)]
    return sum(sideways(groups[b], b, span) for b in range(3))


def carried(window, previous):
    if previous is None:
        return window
    row = iota(window.shape, 0)
    return window + jnp.where(row < 2, pltpu.roll(previous, 2, 0), 0.0)


def middle_kernel(window_ref, near_ref, first_ref, second_ref, shift_ref, out_ref, taps_ref, sum_ref):
    re = [window_ref[s, 0].astype(F32) for s in range(3)]
    im = [window_ref[s, 1].astype(F32) for s in range(3)]
    gap = iota((COLS, COLS), 0) - iota((COLS, COLS), 1) + BOX_RG // 2
    band = ((gap >= 0) & (gap < BOX_RG)).astype(BF16)
    planes = jnp.concatenate(products(re, im), axis=0)
    summed = matmul(jnp.concatenate(halves(planes), axis=1), jnp.concatenate([band, band], axis=0))
    live = 8 * BLOCKS
    boxed = [sum_rows(summed[ROWS * k : ROWS * k + ROWS], near_ref)[:live] for k in range(9)]
    log_ref = jnp.log(boxed[0] + EPSILON)
    shared = mean_log(boxed[0], window_rows((live, COLS), 0))
    store_shared(shared, [taps_ref.at[d] for d in range(2)], COLS)
    for d in range(2):
        store_taps(features(boxed[0], log_ref, boxed[1 + 4 * d : 5 + 4 * d]), taps_ref.at[d], COLS)

    def keep(j):
        def masked(hidden):
            if j < BLOCKS - 1:
                return hidden
            row = iota(hidden.shape, 0)
            return jnp.where(row < (ROWS - STEP * j) * HIDDEN, hidden, 0.0)

        return masked

    for d in range(2):
        previous = [None, None]
        for j in range(BLOCKS):
            parts = head_block(taps_ref[d, j], first_ref, second_ref, keep(j))
            for o in range(2):
                previous[o] = carried(class_window(parts, o, COLS), previous[o])
                sum_ref[d, o, STEP * j + 7 : STEP * j + 15, :] = previous[o]
        for o in range(2):
            shift = jnp.concatenate([shift_ref[o], shift_ref[o]], axis=1)
            for k in range(8):
                out_ref[d, o, 8 * k : 8 * k + 8, :] = sum_ref[d, o, 8 * k + 8 : 8 * k + 16, :] + shift


def edge_kernel(
    place_ref, window_ref, before_ref, after_ref, near_ref, first_ref, second_ref, shift_ref, done_ref,
    out_ref, taps_ref, sum_ref,
):
    lane = iota((ROWS, 128), 1)
    before, after = before_ref[...].astype(F32), after_ref[...].astype(F32)

    def pixels(slot, part):
        k = 2 * slot + part
        value = window_ref[slot, part].astype(F32)
        own_first = pltpu.roll(value[:, :128], EDGE, 1)
        own_last = pltpu.roll(value[:, 128:], 96, 1)
        left = pltpu.roll(before, 128 - EDGE * k, 1) if k else before
        right = pltpu.roll(after, 96 - EDGE * k, 1)
        tile = jnp.where(lane < EDGE, left, own_first)
        tile = jnp.where(lane < 64, tile, own_last)
        tile = jnp.where(lane < 96, tile, right)
        return jnp.where(lane < 112, tile, 0.0)

    planes = products([pixels(s, 0) for s in range(3)], [pixels(s, 1) for s in range(3)])
    source, target = iota((128, 128), 0), iota((128, 128), 1)
    from_col = jnp.where(source < 64, source - 16, source + 160)
    side = target % 64 // 32
    to_col = target % 32 + jnp.where(side == 0, -4, 232)
    gap = from_col - to_col + BOX_RG // 2
    near = (gap >= 0) & (gap < BOX_RG) & (source // 64 == side)
    bands = [(near & (target // 64 == d)).astype(BF16) for d in range(2)]
    band = jnp.concatenate([bands[0], bands[0], bands[1], bands[1]], axis=0)
    dates = [jnp.concatenate([planes[0]] + planes[1 + 4 * d : 5 + 4 * d], axis=0) for d in range(2)]
    summed = matmul(jnp.concatenate(halves(dates[0]) + halves(dates[1]), axis=1), band)

    def paired(value):
        return jnp.concatenate([value[:48], value[48:]], axis=1)

    boxed = [paired(sum_rows(summed[ROWS * k : ROWS * k + ROWS], near_ref)) for k in range(5)]
    place = place_ref[0]

    def in_frame(rows):
        spot = iota((rows, COLS), 1)
        column = spot % 32 + jnp.where(spot % 64 < 32, -4, 232)
        low = jnp.where(place == 0, 0, -128)
        high = jnp.where(place == place_ref[1] - 1, COLS, 2 * COLS)
        return (column >= low) & (column < high)

    valid = in_frame(48)
    base = jnp.where(iota((48, COLS), 1) < 128, 0, STEP * BLOCKS // 2 + 3)
    shared = mean_log(boxed[0], window_rows((48, COLS), base) & valid)
    store_shared(shared, [taps_ref], 128)
    taken = features(boxed[0], jnp.log(boxed[0] + EPSILON), boxed[1:])
    store_taps([jnp.where(valid, f, 0.0) for f in taken], taps_ref, 128)
    kept = in_frame(WIDE)
    row, spot = iota((WIDE, COLS), 0), iota((WIDE, COLS), 1)
    ended = kept & ((spot < 128) | (row < 4 * HIDDEN))
    sum_ref[...] = jnp.zeros_like(sum_ref)
    previous = [None, None]
    for j in range(6):
        masked = lambda hidden: jnp.where(ended if j == 4 else kept, hidden, 0.0)
        parts = head_block(taps_ref[j], first_ref, second_ref, masked)
        for o in range(2):
            previous[o] = carried(class_window(parts, o, 128), previous[o])
            at = STEP * j + 7
            sum_ref[o, at : at + 8, :128] = previous[o][:, :128]
            sum_ref[o, at + 36 : at + 44, 128:] = previous[o][:, 128:]
    spot = iota((8, 128), 1)
    for k in range(8):
        at, to = slice(8 * k + 8, 8 * k + 16), slice(8 * k, 8 * k + 8)
        for o in range(2):
            value = sum_ref[o, at, :128] + sum_ref[o, at, 128:] + shift_ref[o]
            for d in range(2):
                left = pltpu.roll(value, 128 - 64 * d - 4, 1)
                right = pltpu.roll(value, (112 - 64 * d - 40) % 128, 1)
                out_ref[d, o, to, :128] = jnp.where(spot < EDGE, left, done_ref[d, o, to, :128])
                out_ref[d, o, to, 128:] = jnp.where(spot >= 112, right, done_ref[d, o, to, 128:])


def vmem():
    return pl.BlockSpec(memory_space=pltpu.VMEM)


def smem():
    return pl.BlockSpec(memory_space=pltpu.SMEM)


def small(mib):
    return pltpu.CompilerParams(vmem_limit_bytes=mib << 20)


def local(
    slave_complex_pixels,
    along_track_line_groups,
    master_epoch_position,
    sweep_identifier,
    initial_filter_kernel,
    initial_filter_shift,
    latter_filter_kernel,
    latter_filter_shift,
):
    date_index = lax.axis_index("date")
    rng_count = lax.axis_size("rng")
    chosen = master_epoch_position[0]
    sent = pl.pallas_call(
        send_kernel,
        out_shape=jax.ShapeDtypeStruct((BANDS, 3, 2, 8, COLS), BF16),
        in_specs=[smem(), vmem()],
        out_specs=vmem(),
        compiler_params=small(4),
    )(master_epoch_position, slave_complex_pixels.reshape(BANDS, 2, 2, 8, COLS))
    bands = lax.all_to_all(sent, "date", split_axis=0, concat_axis=0, tiled=True)

    lists = along_track_line_groups[:, 0, :]
    mine = lax.dynamic_slice_in_dim(lists, date_index * 2, 2, 0)
    lists = jnp.concatenate([mine, lax.dynamic_slice_in_dim(lists, chosen, 1, 0)], axis=0)
    row_of = lax.broadcasted_iota(jnp.int32, (3, ROWS, 8 * BANDS), 2)
    picks = (lists[:, :, None] == row_of).astype(BF16)

    window = jnp.arange(8 * WINDOWS)
    frame_row = window // 8 * STEP - 1 + window % 8
    row_id = jnp.arange(ROWS)
    burst = sweep_identifier.astype(jnp.int32)
    target_burst = jnp.sum(jnp.where(frame_row[:, None] == row_id[None, :], burst[None, :], 0), axis=1)
    near = (
        (jnp.abs(row_id[None, :] - frame_row[:, None]) <= BOX_AZ // 2)
        & (burst[None, :] == target_burst[:, None])
        & (frame_row >= 0)[:, None]
        & (frame_row < ROWS)[:, None]
    ).astype(BF16)
    near = jnp.concatenate([near, near], axis=1)

    first = jnp.concatenate(
        [
            initial_filter_kernel.reshape(HIDDEN, 45),
            initial_filter_shift[:, None],
            jnp.zeros((HIDDEN, 2), F32),
        ],
        axis=1,
    )
    second = jnp.pad(
        jnp.transpose(latter_filter_kernel, (2, 3, 0, 1)).reshape(18, HIDDEN), ((0, 6), (0, 0))
    )
    first_spread, second_spread, shift = pl.pallas_call(
        spread_kernel,
        out_shape=(
            jax.ShapeDtypeStruct((2 * WIDE, COLS), BF16),
            jax.ShapeDtypeStruct((96, WIDE), BF16),
            jax.ShapeDtypeStruct((2, 8, 128), F32),
        ),
        in_specs=[vmem()] * 2 + [smem()],
        out_specs=(vmem(),) * 3,
        compiler_params=small(8),
        cost_estimate=pl.CostEstimate(flops=10**7, bytes_accessed=10**6, transcendentals=0),
    )(first, second, latter_filter_shift)

    pixels, first_edge, last_edge = pl.pallas_call(
        pick_kernel,
        out_shape=(
            jax.ShapeDtypeStruct((3, 2, ROWS, COLS), BF16),
            jax.ShapeDtypeStruct((ROWS, 128), BF16),
            jax.ShapeDtypeStruct((ROWS, 128), BF16),
        ),
        in_specs=[vmem()] * 2,
        out_specs=(vmem(),) * 3,
        compiler_params=small(8),
    )(picks, bands)

    up = [(i, i + 1) for i in range(rng_count - 1)]
    down = [(i + 1, i) for i in range(rng_count - 1)]
    before = lax.ppermute(last_edge, "rng", up)
    after = lax.ppermute(first_edge, "rng", down)

    middle = pl.pallas_call(
        middle_kernel,
        out_shape=jax.ShapeDtypeStruct((2, 2, ROWS, COLS), F32),
        in_specs=[vmem()] * 5,
        out_specs=vmem(),
        scratch_shapes=[
            pltpu.VMEM((2, BLOCKS, 256, COLS), BF16),
            pltpu.VMEM((2, 2, 80, COLS), F32),
        ],
        compiler_params=small(16),
        cost_estimate=pl.CostEstimate(flops=4 * 10**9, bytes_accessed=10**7, transcendentals=10**5),
    )(pixels, near, first_spread, second_spread, shift)

    place = jnp.stack([lax.axis_index("rng"), jnp.int32(rng_count)]).astype(jnp.int32)
    return pl.pallas_call(
        edge_kernel,
        out_shape=jax.ShapeDtypeStruct((2, 2, ROWS, COLS), F32),
        in_specs=[smem()] + [vmem()] * 8,
        out_specs=vmem(),
        scratch_shapes=[
            pltpu.VMEM((6, 256, COLS), BF16),
            pltpu.VMEM((2, 88, COLS), F32),
        ],
        compiler_params=small(16),
    )(place, pixels, before, after, near, first_spread, second_spread, shift, middle)


def solution(mesh):
    placed = (P(None, None, "date", "rng"), P(None, "rng", None), P(), P(), P(), P(), P(), P())
    return jax.shard_map(
        local, mesh=mesh, in_specs=placed, out_specs=P("date", None, None, "rng"), check_vma=False
    )
```

time: 49.6 us -> 39.1 us (0.79)
  Pallas kernels: 20.7 us -> 12.8 us
  other arithmetic: 4.77 us -> 0.64 us
  waiting for transfers between devices: 3.6 us -> 5.05 us
    pallas_call x1, Pallas kernels: 10.1 us -> 6.79 us  [local(): pl.pallas_call(middle_kernel, out_shape=jax.ShapeDtypeStruct((2, 2, ROWS,...]
    pallas_call x1, Pallas kernels: 6.37 us -> 3.63 us  [local(): pl.pallas_call(edge_kernel, out_shape=jax.ShapeDtypeStruct((2, 2, ROWS, C...]
    concatenate x2 -> x1, other arithmetic: 2.42 us -> 0.08 us  [local(): jnp.concatenate([initial_filter_kernel.reshape(HIDDEN, 45), initial_filte...]
    pallas_call x1, Pallas kernels: 1.91 us -> 0.27 us  [local(): pl.pallas_call(pick_kernel, out_shape=(jax.ShapeDtypeStruct((3, 2, ROWS,...]
    unnamed x16 -> x14, local copies, waits for them, and re-layouts: 2.61 us -> 4.09 us
    all_to_all x1, waiting for transfers between devices: 3.59 us -> 5.05 us  [local(): lax.all_to_all(sent, 'date', split_axis=0, concat_axis=0, tiled=True)]
    broadcast_in_dim x3 -> x1, local copies, waits for them, and re-layouts: 0.72 us -> 0.01 us  [local(): jnp.zeros((HIDDEN, 2), F32)]
    convert_element_type x1, other arithmetic: 0.71 us -> 0.09 us  [local(): picks = (lists[:, :, None] == row_of).astype(BF16)]
  transfers between devices with their start and end apart: 3 -> 3, of which waited for: 1 -> 1; matrix products, arithmetic and copies ran while one was open for 8% -> 2% of each run, Pallas kernels for 25% -> 21%
where the time goes in v2:
time: 39.1 us; the launch traced here: 38.7 us
  starting transfers between devices  15 us (38%)
  Pallas kernels  12.8 us (33%)
  waiting for transfers between devices  5.05 us (13%)
  local copies, waits for them, and re-layouts  4.38 us (11%)
  between operations  0.86 us (2%)
  other arithmetic  0.64 us (2%)
    all_to_all x1, starting transfers between devices, local(): lax.all_to_all(sent, 'date', split_axis=0, concat_axis=0, tiled=True)  7.03 us
    pallas_call x1, Pallas kernels, local(): pl.pallas_call(middle_kernel, out_shape=jax.ShapeDtypeStruct((2, 2, ROWS,...  6.79 us
    ppermute x1, starting transfers between devices, local(): after = lax.ppermute(first_edge, 'rng', down)  5.37 us
    all_to_all x1, waiting for transfers between devices, local(): lax.all_to_all(sent, 'date', split_axis=0, concat_axis=0, tiled=True)  5.05 us
    unnamed x14, local copies, waits for them, and re-layouts  4.09 us
    pallas_call x1, Pallas kernels, local(): pl.pallas_call(edge_kernel, out_shape=jax.ShapeDtypeStruct((2, 2, ROWS, C...  3.63 us
    ppermute x1, starting transfers between devices, local(): before = lax.ppermute(last_edge, 'rng', up)  2.58 us
    pallas_call x1, Pallas kernels, local(): pl.pallas_call(spread_kernel, out_shape=(jax.ShapeDtypeStruct((2 * WIDE,...  1.32 us
  transfers between devices with their start and end apart: 3, of which 1 were waited for; matrix products, arithmetic and copies ran while one was open for 2% of the time, Pallas kernels for 21%

profile of v2, /device:TPU:128, one launch (start us, length us, event | category | flops | bytes accessed | tf_op | source)
XLA Modules:
  0.0 38.7 jit_solution(11189844157574568457)
XLA Ops:
  0.0 0.0 copy-start
  0.7 0.0 copy-start.1
  0.7 0.9 %copy-done.1 = bf16[32,2,8,256]{3,2,1,0:T(8,128)(2,1)S(1)} copy-done((bf16[32,2,8,256]{3,2,1,0:T(8,128)(2,1)S(1)}, bf16[32,2,8,256]{3,2,1,0:T(8,128)(2,1)}, u32[]{:S(2)}) %copy-start.1) | copy-done | bytes 262168
  1.6 0.8 %shard_map.82 = bf16[16,3,2,8,256]{4,3,2,1,0:T(8,128)(2,1)} custom-call(s32[1]{0:T(128)} %copy.13.chosen_ref, bf16[16,2,2,8,256]{4,3,2,1,0:T(8,128)(2,1)S(1)} %bitcast.13), custom_call_target="tpu_custom_call" | custom-call | tf_op jit(solution)/shard_map/pallas_call | solution.py:325
  2.4 7.0 %all-to-all-start = ((bf16[16,3,2,8,256]{4,3,2,1,0:T(8,128)(2,1)}), bf16[16,3,2,8,256]{4,3,2,1,0:T(8,128)(2,1)S(1)}, u32[]{:S(2)}, u32[]{:S(2)}) async-start(bf16[16,3,2,8,256]{4,3,2,1,0:T(8,128)(2,1)} %shard_map.82), calls=%async_computation | async-start | bytes 786432 | tf_op jit(solution)/shard_map/all_to_all | solution.py:332
  9.4 0.0 copy-start.3
  9.5 0.0 copy-done
  9.5 0.7 %copy-done.3 = f32[32,5,3,3]{0,3,2,1:T(4,128)S(1)} copy-done((f32[32,5,3,3]{0,3,2,1:T(4,128)S(1)}, f32[32,5,3,3]{0,3,2,1:T(4,128)}, u32[]{:S(2)}) %copy-start.3) | copy-done | bytes 5784
  10.2 0.1 copy.11
  10.3 0.0 copy-start.5
  10.3 0.7 %copy-done.5 = f32[32]{0:T(128)S(1)} copy-done((f32[32]{0:T(128)S(1)}, f32[32]{0:T(128)}, u32[]{:S(2)}) %copy-start.5) | copy-done | bytes 152
  10.9 0.1 copy.12
  11.0 0.0 copy-start.6
  11.0 0.6 %copy-done.6 = s32[64]{0:T(128)S(1)} copy-done((s32[64]{0:T(128)S(1)}, s32[64]{0:T(128)}, u32[]{:S(2)}) %copy-start.6) | copy-done | bytes 280
  11.7 0.2 select_reduce_fusion
  11.9 0.1 pad.7.clone
  11.9 0.1 fusion.3
  12.1 0.0 copy-start.4
  12.1 0.1 maximum_maximum_fusion.first_ref
  12.2 0.1 pad_add_fusion.1.place_ref
  12.2 0.5 %copy-done.4 = f32[2,32,3,3]{1,0,3,2:T(2,128)S(1)} copy-done((f32[2,32,3,3]{1,0,3,2:T(2,128)S(1)}, f32[2,32,3,3]{1,0,3,2:T(2,128)}, u32[]{:S(2)}) %copy-start.4) | copy-done | bytes 2328
  12.8 0.0 copy-start.2
  12.8 0.6 %copy-done.2 = f32[2]{0:T(128)S(1)} copy-done((f32[2]{0:T(128)S(1)}, f32[2]{0:T(128)}, u32[]{:S(2)}) %copy-start.2) | copy-done | bytes 32
  13.4 1.3 %shard_map.84 = (bf16[384,256]{1,0:T(8,128)(2,1)S(1)}, bf16[96,192]{1,0:T(8,128)(2,1)S(1)}, f32[2,8,128]{2,1,0:T(8,128)S(1)}) custom-call(f32[32,48]{1,0:T(8,128)S(1)} %maximum_maximum_fusion.first_ref, f32[24,32]{1,0:T(8,128)S(1)} %pad.4.second_ref, f32[2]{0:T(128)S(1)} %copy-done.2), custom_call_target="tpu_custom_call" | custom-call | flops 10000000 | bytes 1000000 | tf_op jit(solution)/shard_map/pallas_call | solution.py:364
  14.8 0.1 add_convert_fusion.near_ref
  14.9 0.1 fusion.chosen_ref
  15.0 5.0 %all-to-all-done.bands_ref = bf16[16,3,2,8,256]{4,3,2,1,0:T(8,128)(2,1)S(1)} async-done(((bf16[16,3,2,8,256]{4,3,2,1,0:T(8,128)(2,1)}), bf16[16,3,2,8,256]{4,3,2,1,0:T(8,128)(2,1)S(1)}, u32[]{:S(2)}, u32[]{:S(2)}) %all-to-all-start) | async-done | bytes 393248 | tf_op jit(solution)/shard_map/all_to_all | solution.py:332
  20.0 0.3 shard_map.83
  20.3 2.6 %collective-permute-start = (bf16[64,128]{1,0:T(8,128)(2,1)S(1)}, bf16[64,128]{1,0:T(8,128)(2,1)S(1)}, u32[]{:S(2)}, u32[]{:S(2)}) collective-permute-start(bf16[64,128]{1,0:T(8,128)(2,1)S(1)} %get-tuple-element.12), channel_id=1, source_target_pairs={{0,1},{1,2},{2,3},{3,4},{4,5},{5,6},{6,7},{7,8},{8,9},{9,10},{10,1... | collective-permute-start | bytes 49160 | tf_op jit(solution)/shard_map/ppermute | solution.py:391
  22.9 5.4 %collective-permute-start.1 = (bf16[64,128]{1,0:T(8,128)(2,1)S(1)}, bf16[64,128]{1,0:T(8,128)(2,1)S(1)}, u32[]{:S(2)}, u32[]{:S(2)}) collective-permute-start(bf16[64,128]{1,0:T(8,128)(2,1)S(1)} %get-tuple-element.13), channel_id=1, source_target_pairs={{1,0},{2,1},{3,2},{4,3},{5,4},{6,5},{7,6},{8,7},{9,8},{10,9},{11,1... | collective-permute-start | bytes 49160 | tf_op jit(solution)/shard_map/ppermute | solution.py:392
  28.3 6.8 %shard_map.85.done_ref = f32[2,2,64,256]{3,2,1,0:T(8,128)S(1)} custom-call(bf16[3,2,64,256]{3,2,1,0:T(8,128)(2,1)S(1)} %get-tuple-element.11.window_ref, bf16[96,128]{1,0:T(8,128)(2,1)S(1)} %add_convert_fusion.near_ref, bf16[384,256]{1,0:T(8,128)(2,1)S(1)} %get-tuple-element.14.first_ref, bf16[96,192]{1,0:T(8,128)(2,1)S(1)} %get-tuple-element.15.second_ref, ...), custom_call_target="tpu_custom_call" | custom-call | flops 4000000000 | bytes 10000000 | tf_op jit(solution)/shard_map/pallas_call | solution.py:394
  35.1 0.0 collective-permute-done.before_ref
  35.1 0.0 collective-permute-done.1.after_ref
  35.1 3.6 %shard_map.86 = f32[2,2,64,256]{3,2,1,0:T(8,128)} custom-call(s32[2]{0:T(128)S(1)} %pad_add_fusion.1.place_ref, bf16[3,2,64,256]{3,2,1,0:T(8,128)(2,1)S(1)} %get-tuple-element.11.window_ref, bf16[64,128]{1,0:T(8,128)(2,1)S(1)} %collective-permute-done.before_ref, bf16[64,128]{1,0:T(8,128)(2,1)S(1)} %collective-permute-done.1.after_ref, ...), custom_call_target="tpu_custom_call" | custom-call | tf_op jit(solution)/shard_map/pallas_call | solution.py:408
  (9 shorter events, 0.1 us)
Async XLA Ops:
  0.0 9.5 %copy-start = (s32[32,1,64]{2,1,0:T(1,128)S(1)}, s32[32,1,64]{2,1,0:T(1,128)}, u32[]{:S(2)}) copy-start(s32[32,1,64]{2,1,0:T(1,128)} %param.9) | copy-start | bytes 24580
  0.7 1.0 %copy-start.1 = (bf16[32,2,8,256]{3,2,1,0:T(8,128)(2,1)S(1)}, bf16[32,2,8,256]{3,2,1,0:T(8,128)(2,1)}, u32[]{:S(2)}) copy-start(bf16[32,2,8,256]{3,2,1,0:T(8,128)(2,1)} %param.8) | copy-start | bytes 786436
  2.4 17.6 %all-to-all-start = ((bf16[16,3,2,8,256]{4,3,2,1,0:T(8,128)(2,1)}), bf16[16,3,2,8,256]{4,3,2,1,0:T(8,128)(2,1)S(1)}, u32[]{:S(2)}, u32[]{:S(2)}) async-start(bf16[16,3,2,8,256]{4,3,2,1,0:T(8,128)(2,1)} %shard_map.82), calls=%async_computation | async-start | bytes 786432 | tf_op jit(solution)/shard_map/all_to_all | solution.py:332
  9.4 0.8 %copy-start.3 = (f32[32,5,3,3]{0,3,2,1:T(4,128)S(1)}, f32[32,5,3,3]{0,3,2,1:T(4,128)}, u32[]{:S(2)}) copy-start(f32[32,5,3,3]{0,3,2,1:T(4,128)} %param.12) | copy-start | bytes 17284
  10.3 0.7 %copy-start.5 = (f32[32]{0:T(128)S(1)}, f32[32]{0:T(128)}, u32[]{:S(2)}) copy-start(f32[32]{0:T(128)} %param.13) | copy-start | bytes 388
  11.0 0.7 %copy-start.6 = (s32[64]{0:T(128)S(1)}, s32[64]{0:T(128)}, u32[]{:S(2)}) copy-start(s32[64]{0:T(128)} %param.11) | copy-start | bytes 772
  12.1 0.7 %copy-start.4 = (f32[2,32,3,3]{1,0,3,2:T(2,128)S(1)}, f32[2,32,3,3]{1,0,3,2:T(2,128)}, u32[]{:S(2)}) copy-start(f32[2,32,3,3]{1,0,3,2:T(2,128)} %param.14) | copy-start | bytes 6916
  12.8 0.7 %copy-start.2 = (f32[2]{0:T(128)S(1)}, f32[2]{0:T(128)}, u32[]{:S(2)}) copy-start(f32[2]{0:T(128)} %shift_ref.1) | copy-start | bytes 28
  20.3 14.8 %collective-permute-start = (bf16[64,128]{1,0:T(8,128)(2,1)S(1)}, bf16[64,128]{1,0:T(8,128)(2,1)S(1)}, u32[]{:S(2)}, u32[]{:S(2)}) collective-permute-start(bf16[64,128]{1,0:T(8,128)(2,1)S(1)} %get-tuple-element.12), channel_id=1, source_target_pairs={{0,1},{1,2},{2,3},{3,4},{4,5},{5,6},{6,7},{7,8},{8,9},{9,10},{10,1... | collective-permute-start | bytes 49160 | tf_op jit(solution)/shard_map/ppermute | solution.py:391
  22.9 12.2 %collective-permute-start.1 = (bf16[64,128]{1,0:T(8,128)(2,1)S(1)}, bf16[64,128]{1,0:T(8,128)(2,1)S(1)}, u32[]{:S(2)}, u32[]{:S(2)}) collective-permute-start(bf16[64,128]{1,0:T(8,128)(2,1)S(1)} %get-tuple-element.13), channel_id=1, source_target_pairs={{1,0},{2,1},{3,2},{4,3},{5,4},{6,5},{7,6},{8,7},{9,8},{10,9},{11,1... | collective-permute-start | bytes 49160 | tf_op jit(solution)/shard_map/ppermute | solution.py:392

commit v3 on v2

--- a/solution.py
+++ b/solution.py
@@ -165,10 +165,13 @@
         store_pieces(taps_ref, 14, moved[2], one)
 
 
-def head_block(taps, first_ref, second_ref, keep):
+def first_part(taps, first_ref):
     doubled = matmul(first_ref[...], taps)
-    hidden = jnp.maximum(doubled[:WIDE] + doubled[WIDE:], 0.0)
-    high, low = halves(keep(hidden))
+    return doubled[:WIDE] + doubled[WIDE:]
+
+
+def second_part(sums, second_ref, keep):
+    high, low = halves(keep(jnp.maximum(sums, 0.0)))
     doubled = matmul(second_ref[...], high)
     return doubled[:48] + doubled[48:] + matmul(second_ref[:48, :], low)
 
@@ -196,9 +199,10 @@
     boxed = [sum_rows(summed[ROWS * k : ROWS * k + ROWS], near_ref)[:live] for k in range(9)]
     log_ref = jnp.log(boxed[0] + EPSILON)
     shared = mean_log(boxed[0], window_rows((live, COLS), 0))
-    store_shared(shared, [taps_ref.at[d] for d in range(2)], COLS)
+    sides = [taps_ref.at[:, :, COLS * d : COLS * d + COLS] for d in range(2)]
+    store_shared(shared, sides, COLS)
     for d in range(2):
-        store_taps(features(boxed[0], log_ref, boxed[1 + 4 * d : 5 + 4 * d]), taps_ref.at[d], COLS)
+        store_taps(features(boxed[0], log_ref, boxed[1 + 4 * d : 5 + 4 * d]), sides[d], COLS)
 
     def keep(j):
         def masked(hidden):
@@ -209,17 +213,21 @@
 
         return masked
 
+    previous = [None, None]
+    ahead = first_part(taps_ref[0], first_ref)
+    for j in range(BLOCKS):
+        later = first_part(taps_ref[j + 1], first_ref) if j + 1 < BLOCKS else None
+        parts = second_part(ahead, second_ref, keep(j))
+        ahead = later
+        for o in range(2):
+            previous[o] = carried(class_window(parts, o, COLS), previous[o])
+            sum_ref[o, STEP * j + 7 : STEP * j + 15, :] = previous[o]
     for d in range(2):
-        previous = [None, None]
-        for j in range(BLOCKS):
-            parts = head_block(taps_ref[d, j], first_ref, second_ref, keep(j))
-            for o in range(2):
-                previous[o] = carried(class_window(parts, o, COLS), previous[o])
-                sum_ref[d, o, STEP * j + 7 : STEP * j + 15, :] = previous[o]
         for o in range(2):
             shift = jnp.concatenate([shift_ref[o], shift_ref[o]], axis=1)
             for k in range(8):
-                out_ref[d, o, 8 * k : 8 * k + 8, :] = sum_ref[d, o, 8 * k + 8 : 8 * k + 16, :] + shift
+                done = sum_ref[o, 8 * k + 8 : 8 * k + 16, COLS * d : COLS * d + COLS]
+                out_ref[d, o, 8 * k : 8 * k + 8, :] = done + shift
 
 
 def edge_kernel(
@@ -227,7 +235,9 @@
     out_ref, taps_ref, sum_ref,
 ):
     lane = iota((ROWS, 128), 1)
-    before, after = before_ref[...].astype(F32), after_ref[...].astype(F32)
+    place = place_ref[0]
+    before = jnp.where(place == 0, 0.0, before_ref[...].astype(F32))
+    after = jnp.where(place == place_ref[1] - 1, 0.0, after_ref[...].astype(F32))
 
     def pixels(slot, part):
         k = 2 * slot + part
@@ -253,43 +263,45 @@
     dates = [jnp.concatenate([planes[0]] + planes[1 + 4 * d : 5 + 4 * d], axis=0) for d in range(2)]
     summed = matmul(jnp.concatenate(halves(dates[0]) + halves(dates[1]), axis=1), band)
 
-    def paired(value):
-        return jnp.concatenate([value[:48], value[48:]], axis=1)
-
-    boxed = [paired(sum_rows(summed[ROWS * k : ROWS * k + ROWS], near_ref)) for k in range(5)]
-    place = place_ref[0]
+    def spread(value):
+        return jnp.concatenate([value[24 * q : 24 * q + 24] for q in range(4)], axis=1)
+
+    boxed = [spread(sum_rows(summed[ROWS * k : ROWS * k + ROWS], near_ref)) for k in range(5)]
 
     def in_frame(rows):
-        spot = iota((rows, COLS), 1)
+        spot = iota((rows, 512), 1)
         column = spot % 32 + jnp.where(spot % 64 < 32, -4, 232)
         low = jnp.where(place == 0, 0, -128)
         high = jnp.where(place == place_ref[1] - 1, COLS, 2 * COLS)
         return (column >= low) & (column < high)
 
-    valid = in_frame(48)
-    base = jnp.where(iota((48, COLS), 1) < 128, 0, STEP * BLOCKS // 2 + 3)
-    shared = mean_log(boxed[0], window_rows((48, COLS), base) & valid)
+    valid = in_frame(24)
+    base = iota((24, 512), 1) // 128 * (3 * STEP)
+    shared = mean_log(boxed[0], window_rows((24, 512), base) & valid)
     store_shared(shared, [taps_ref], 128)
     taken = features(boxed[0], jnp.log(boxed[0] + EPSILON), boxed[1:])
     store_taps([jnp.where(valid, f, 0.0) for f in taken], taps_ref, 128)
     kept = in_frame(WIDE)
-    row, spot = iota((WIDE, COLS), 0), iota((WIDE, COLS), 1)
-    ended = kept & ((spot < 128) | (row < 4 * HIDDEN))
+    row, spot = iota((WIDE, 512), 0), iota((WIDE, 512), 1)
+    ended = kept & ((spot < 384) | (row < 4 * HIDDEN))
     sum_ref[...] = jnp.zeros_like(sum_ref)
     previous = [None, None]
-    for j in range(6):
-        masked = lambda hidden: jnp.where(ended if j == 4 else kept, hidden, 0.0)
-        parts = head_block(taps_ref[j], first_ref, second_ref, masked)
+    ahead = first_part(taps_ref[0], first_ref)
+    for j in range(3):
+        later = first_part(taps_ref[j + 1], first_ref) if j < 2 else None
+        mask = ended if j == 1 else kept
+        parts = second_part(ahead, second_ref, lambda hidden: jnp.where(mask, hidden, 0.0))
+        ahead = later
         for o in range(2):
             previous[o] = carried(class_window(parts, o, 128), previous[o])
-            at = STEP * j + 7
-            sum_ref[o, at : at + 8, :128] = previous[o][:, :128]
-            sum_ref[o, at + 36 : at + 44, 128:] = previous[o][:, 128:]
+            for q in range(4):
+                at, lanes = STEP * (j + 3 * q) + 7, slice(128 * q, 128 * q + 128)
+                sum_ref[o, at : at + 8, lanes] = previous[o][:, lanes]
     spot = iota((8, 128), 1)
     for k in range(8):
         at, to = slice(8 * k + 8, 8 * k + 16), slice(8 * k, 8 * k + 8)
         for o in range(2):
-            value = sum_ref[o, at, :128] + sum_ref[o, at, 128:] + shift_ref[o]
+            value = sum(sum_ref[o, at, 128 * q : 128 * q + 128] for q in range(4)) + shift_ref[o]
             for d in range(2):
                 left = pltpu.roll(value, 128 - 64 * d - 4, 1)
                 right = pltpu.roll(value, (112 - 64 * d - 40) % 128, 1)
@@ -386,8 +398,8 @@
         compiler_params=small(8),
     )(picks, bands)
 
-    up = [(i, i + 1) for i in range(rng_count - 1)]
-    down = [(i + 1, i) for i in range(rng_count - 1)]
+    up = [(i, (i + 1) % rng_count) for i in range(rng_count)]
+    down = [(j, i) for i, j in up]
     before = lax.ppermute(last_edge, "rng", up)
     after = lax.ppermute(first_edge, "rng", down)
 
@@ -397,8 +409,8 @@
         in_specs=[vmem()] * 5,
         out_specs=vmem(),
         scratch_shapes=[
-            pltpu.VMEM((2, BLOCKS, 256, COLS), BF16),
-            pltpu.VMEM((2, 2, 80, COLS), F32),
+            pltpu.VMEM((BLOCKS, 256, 2 * COLS), BF16),
+            pltpu.VMEM((2, 80, 2 * COLS), F32),
         ],
         compiler_params=small(16),
         cost_estimate=pl.CostEstimate(flops=4 * 10**9, bytes_accessed=10**7, transcendentals=10**5),
@@ -411,8 +423,8 @@
         in_specs=[smem()] + [vmem()] * 8,
         out_specs=vmem(),
         scratch_shapes=[
-            pltpu.VMEM((6, 256, COLS), BF16),
-            pltpu.VMEM((2, 88, COLS), F32),
+            pltpu.VMEM((3, 256, 512), BF16),
+            pltpu.VMEM((2, 88, 512), F32),
         ],
         compiler_params=small(16),
     )(place, pixels, before, after, near, first_spread, second_spread, shift, middle)

time: 39.1 us -> 33.1 us (0.85)
  the two profiles are of different devices: /device:TPU:128 before, /device:TPU:1 now
where the time goes in v3:
time: 33.1 us; the launch traced here: 32.8 us
  starting transfers between devices  14.3 us (43%)
  Pallas kernels  8.05 us (24%)
  waiting for transfers between devices  4.58 us (14%)
  local copies, waits for them, and re-layouts  4.38 us (13%)
  between operations  0.83 us (3%)
  other arithmetic  0.64 us (2%)
    all_to_all x1, starting transfers between devices, local(): lax.all_to_all(sent, 'date', split_axis=0, concat_axis=0, tiled=True)  8.44 us
    ppermute x1, starting transfers between devices, local(): after = lax.ppermute(first_edge, 'rng', down)  5.38 us
    all_to_all x1, waiting for transfers between devices, local(): lax.all_to_all(sent, 'date', split_axis=0, concat_axis=0, tiled=True)  4.57 us
    unnamed x14, local copies, waits for them, and re-layouts  4.09 us
    pallas_call x1, Pallas kernels, local(): pl.pallas_call(middle_kernel, out_shape=jax.ShapeDtypeStruct((2, 2, ROWS,...  2.88 us
    pallas_call x1, Pallas kernels, local(): pl.pallas_call(edge_kernel, out_shape=jax.ShapeDtypeStruct((2, 2, ROWS, C...  2.81 us
    pallas_call x1, Pallas kernels, local(): pl.pallas_call(spread_kernel, out_shape=(jax.ShapeDtypeStruct((2 * WIDE,...  1.32 us
    pallas_call x1, Pallas kernels, local(): pl.pallas_call(send_kernel, out_shape=jax.ShapeDtypeStruct((BANDS, 3, 2,...  0.77 us
  transfers between devices with their start and end apart: 3, of which 1 were waited for; matrix products, arithmetic and copies ran while one was open for 3% of the time, Pallas kernels for 13%

profile of v3, /device:TPU:1, one launch (start us, length us, event | category | flops | bytes accessed | tf_op | source)
XLA Modules:
  0.0 32.8 jit_solution(7020620200305517288)
XLA Ops:
  0.0 0.0 copy-start
  0.7 0.0 copy-start.1
  0.7 0.9 %copy-done.1 = bf16[32,2,8,256]{3,2,1,0:T(8,128)(2,1)S(1)} copy-done((bf16[32,2,8,256]{3,2,1,0:T(8,128)(2,1)S(1)}, bf16[32,2,8,256]{3,2,1,0:T(8,128)(2,1)}, u32[]{:S(2)}) %copy-start.1) | copy-done | bytes 262168
  1.6 0.8 %shard_map.82 = bf16[16,3,2,8,256]{4,3,2,1,0:T(8,128)(2,1)} custom-call(s32[1]{0:T(128)} %copy.13.chosen_ref, bf16[16,2,2,8,256]{4,3,2,1,0:T(8,128)(2,1)S(1)} %bitcast.13), custom_call_target="tpu_custom_call" | custom-call | tf_op jit(solution)/shard_map/pallas_call | solution.py:337
  2.4 8.4 %all-to-all-start = ((bf16[16,3,2,8,256]{4,3,2,1,0:T(8,128)(2,1)}), bf16[16,3,2,8,256]{4,3,2,1,0:T(8,128)(2,1)S(1)}, u32[]{:S(2)}, u32[]{:S(2)}) async-start(bf16[16,3,2,8,256]{4,3,2,1,0:T(8,128)(2,1)} %shard_map.82), calls=%async_computation | async-start | bytes 786432 | tf_op jit(solution)/shard_map/all_to_all | solution.py:344
  10.8 0.0 copy-start.3
  10.9 0.0 copy-done
  10.9 0.7 %copy-done.3 = f32[32,5,3,3]{0,3,2,1:T(4,128)S(1)} copy-done((f32[32,5,3,3]{0,3,2,1:T(4,128)S(1)}, f32[32,5,3,3]{0,3,2,1:T(4,128)}, u32[]{:S(2)}) %copy-start.3) | copy-done | bytes 5784
  11.6 0.1 copy.11
  11.7 0.0 copy-start.5
  11.7 0.7 %copy-done.5 = f32[32]{0:T(128)S(1)} copy-done((f32[32]{0:T(128)S(1)}, f32[32]{0:T(128)}, u32[]{:S(2)}) %copy-start.5) | copy-done | bytes 152
  12.3 0.1 copy.12
  12.4 0.0 copy-start.6
  12.4 0.6 %copy-done.6 = s32[64]{0:T(128)S(1)} copy-done((s32[64]{0:T(128)S(1)}, s32[64]{0:T(128)}, u32[]{:S(2)}) %copy-start.6) | copy-done | bytes 280
  13.1 0.2 select_reduce_fusion
  13.3 0.1 pad.7.clone
  13.3 0.1 fusion.3
  13.5 0.0 copy-start.4
  13.5 0.1 maximum_maximum_fusion.first_ref
  13.5 0.1 pad_add_fusion.1.place_ref
  13.6 0.5 %copy-done.4 = f32[2,32,3,3]{1,0,3,2:T(2,128)S(1)} copy-done((f32[2,32,3,3]{1,0,3,2:T(2,128)S(1)}, f32[2,32,3,3]{1,0,3,2:T(2,128)}, u32[]{:S(2)}) %copy-start.4) | copy-done | bytes 2328
  14.2 0.0 copy-start.2
  14.2 0.6 %copy-done.2 = f32[2]{0:T(128)S(1)} copy-done((f32[2]{0:T(128)S(1)}, f32[2]{0:T(128)}, u32[]{:S(2)}) %copy-start.2) | copy-done | bytes 32
  14.8 1.3 %shard_map.84 = (bf16[384,256]{1,0:T(8,128)(2,1)S(1)}, bf16[96,192]{1,0:T(8,128)(2,1)S(1)}, f32[2,8,128]{2,1,0:T(8,128)S(1)}) custom-call(f32[32,48]{1,0:T(8,128)S(1)} %maximum_maximum_fusion.first_ref, f32[24,32]{1,0:T(8,128)S(1)} %pad.4.second_ref, f32[2]{0:T(128)S(1)} %copy-done.2), custom_call_target="tpu_custom_call" | custom-call | flops 10000000 | bytes 1000000 | tf_op jit(solution)/shard_map/pallas_call | solution.py:376
  16.2 0.1 add_convert_fusion.near_ref
  16.2 0.1 fusion.chosen_ref
  16.3 4.6 %all-to-all-done.bands_ref = bf16[16,3,2,8,256]{4,3,2,1,0:T(8,128)(2,1)S(1)} async-done(((bf16[16,3,2,8,256]{4,3,2,1,0:T(8,128)(2,1)}), bf16[16,3,2,8,256]{4,3,2,1,0:T(8,128)(2,1)S(1)}, u32[]{:S(2)}, u32[]{:S(2)}) %all-to-all-start) | async-done | bytes 393248 | tf_op jit(solution)/shard_map/all_to_all | solution.py:344
  20.9 0.3 shard_map.83
  21.2 0.5 %collective-permute-start = (bf16[64,128]{1,0:T(8,128)(2,1)S(1)}, bf16[64,128]{1,0:T(8,128)(2,1)S(1)}, u32[]{:S(2)}, u32[]{:S(2)}) collective-permute-start(bf16[64,128]{1,0:T(8,128)(2,1)S(1)} %get-tuple-element.12), channel_id=1, source_target_pairs={{0,1},{1,2},{2,3},{3,4},{4,5},{5,6},{6,7},{7,8},{8,9},{9,10},{10,1... | collective-permute-start | bytes 49160 | tf_op jit(solution)/shard_map/ppermute | solution.py:403
  21.7 5.4 %collective-permute-start.1 = (bf16[64,128]{1,0:T(8,128)(2,1)S(1)}, bf16[64,128]{1,0:T(8,128)(2,1)S(1)}, u32[]{:S(2)}, u32[]{:S(2)}) collective-permute-start(bf16[64,128]{1,0:T(8,128)(2,1)S(1)} %get-tuple-element.13), channel_id=1, source_target_pairs={{1,0},{2,1},{3,2},{4,3},{5,4},{6,5},{7,6},{8,7},{9,8},{10,9},{11,1... | collective-permute-start | bytes 49160 | tf_op jit(solution)/shard_map/ppermute | solution.py:404
  27.1 2.9 %shard_map.85.done_ref = f32[2,2,64,256]{3,2,1,0:T(8,128)S(1)} custom-call(bf16[3,2,64,256]{3,2,1,0:T(8,128)(2,1)S(1)} %get-tuple-element.11.window_ref, bf16[96,128]{1,0:T(8,128)(2,1)S(1)} %add_convert_fusion.near_ref, bf16[384,256]{1,0:T(8,128)(2,1)S(1)} %get-tuple-element.14.first_ref, bf16[96,192]{1,0:T(8,128)(2,1)S(1)} %get-tuple-element.15.second_ref, ...), custom_call_target="tpu_custom_call" | custom-call | flops 4000000000 | bytes 10000000 | tf_op jit(solution)/shard_map/pallas_call | solution.py:406
  29.9 0.0 collective-permute-done.before_ref
  29.9 0.0 collective-permute-done.1.after_ref
  30.0 2.8 %shard_map.86 = f32[2,2,64,256]{3,2,1,0:T(8,128)} custom-call(s32[2]{0:T(128)S(1)} %pad_add_fusion.1.place_ref, bf16[3,2,64,256]{3,2,1,0:T(8,128)(2,1)S(1)} %get-tuple-element.11.window_ref, bf16[64,128]{1,0:T(8,128)(2,1)S(1)} %collective-permute-done.before_ref, bf16[64,128]{1,0:T(8,128)(2,1)S(1)} %collective-permute-done.1.after_ref, ...), custom_call_target="tpu_custom_call" | custom-call | tf_op jit(solution)/shard_map/pallas_call | solution.py:420
  (9 shorter events, 0.1 us)
Async XLA Ops:
  0.0 10.9 %copy-start = (s32[32,1,64]{2,1,0:T(1,128)S(1)}, s32[32,1,64]{2,1,0:T(1,128)}, u32[]{:S(2)}) copy-start(s32[32,1,64]{2,1,0:T(1,128)} %param.9) | copy-start | bytes 24580
  0.7 1.0 %copy-start.1 = (bf16[32,2,8,256]{3,2,1,0:T(8,128)(2,1)S(1)}, bf16[32,2,8,256]{3,2,1,0:T(8,128)(2,1)}, u32[]{:S(2)}) copy-start(bf16[32,2,8,256]{3,2,1,0:T(8,128)(2,1)} %param.8) | copy-start | bytes 786436
  2.4 18.5 %all-to-all-start = ((bf16[16,3,2,8,256]{4,3,2,1,0:T(8,128)(2,1)}), bf16[16,3,2,8,256]{4,3,2,1,0:T(8,128)(2,1)S(1)}, u32[]{:S(2)}, u32[]{:S(2)}) async-start(bf16[16,3,2,8,256]{4,3,2,1,0:T(8,128)(2,1)} %shard_map.82), calls=%async_computation | async-start | bytes 786432 | tf_op jit(solution)/shard_map/all_to_all | solution.py:344
  10.8 0.8 %copy-start.3 = (f32[32,5,3,3]{0,3,2,1:T(4,128)S(1)}, f32[32,5,3,3]{0,3,2,1:T(4,128)}, u32[]{:S(2)}) copy-start(f32[32,5,3,3]{0,3,2,1:T(4,128)} %param.12) | copy-start | bytes 17284
  11.7 0.7 %copy-start.5 = (f32[32]{0:T(128)S(1)}, f32[32]{0:T(128)}, u32[]{:S(2)}) copy-start(f32[32]{0:T(128)} %param.13) | copy-start | bytes 388
  12.4 0.7 %copy-start.6 = (s32[64]{0:T(128)S(1)}, s32[64]{0:T(128)}, u32[]{:S(2)}) copy-start(s32[64]{0:T(128)} %param.11) | copy-start | bytes 772
  13.5 0.7 %copy-start.4 = (f32[2,32,3,3]{1,0,3,2:T(2,128)S(1)}, f32[2,32,3,3]{1,0,3,2:T(2,128)}, u32[]{:S(2)}) copy-start(f32[2,32,3,3]{1,0,3,2:T(2,128)} %param.14) | copy-start | bytes 6916
  14.2 0.7 %copy-start.2 = (f32[2]{0:T(128)S(1)}, f32[2]{0:T(128)}, u32[]{:S(2)}) copy-start(f32[2]{0:T(128)} %shift_ref.1) | copy-start | bytes 28
  21.2 8.7 %collective-permute-start = (bf16[64,128]{1,0:T(8,128)(2,1)S(1)}, bf16[64,128]{1,0:T(8,128)(2,1)S(1)}, u32[]{:S(2)}, u32[]{:S(2)}) collective-permute-start(bf16[64,128]{1,0:T(8,128)(2,1)S(1)} %get-tuple-element.12), channel_id=1, source_target_pairs={{0,1},{1,2},{2,3},{3,4},{4,5},{5,6},{6,7},{7,8},{8,9},{9,10},{10,1... | collective-permute-start | bytes 49160 | tf_op jit(solution)/shard_map/ppermute | solution.py:403
  21.7 8.3 %collective-permute-start.1 = (bf16[64,128]{1,0:T(8,128)(2,1)S(1)}, bf16[64,128]{1,0:T(8,128)(2,1)S(1)}, u32[]{:S(2)}, u32[]{:S(2)}) collective-permute-start(bf16[64,128]{1,0:T(8,128)(2,1)S(1)} %get-tuple-element.13), channel_id=1, source_target_pairs={{1,0},{2,1},{3,2},{4,3},{5,4},{6,5},{7,6},{8,7},{9,8},{10,9},{11,1... | collective-permute-start | bytes 49160 | tf_op jit(solution)/shard_map/ppermute | solution.py:404

commit v4 on v3

--- a/solution.py
+++ b/solution.py
@@ -76,7 +76,8 @@
         shift_out[o] = jnp.full((8, 128), shift_ref[o], F32)
 
 
-def pick_kernel(chosen_ref, bands_ref, window_ref, first_ref, last_ref):
+def pick_kernel(chosen_ref, bands_ref, window_ref, inner_ref, outer_ref):
+    odd = lax.axis_index("rng") % 2 == 1
     lane = iota((ROWS, 128), 1)
     first = jnp.zeros((ROWS, 128), F32)
     last = jnp.zeros((ROWS, 128), F32)
@@ -93,8 +94,8 @@
                 left = pltpu.roll(left, EDGE * k, 1)
             first = jnp.where(here, left, first)
             last = jnp.where(here, right, last)
-    first_ref[...] = first.astype(BF16)
-    last_ref[...] = last.astype(BF16)
+    inner_ref[...] = jnp.where(odd, first, last).astype(BF16)
+    outer_ref[...] = jnp.where(odd, last, first).astype(BF16)
 
 
 def products(re, im):
@@ -231,13 +232,15 @@
 
 
 def edge_kernel(
-    place_ref, window_ref, before_ref, after_ref, near_ref, first_ref, second_ref, shift_ref, done_ref,
+    window_ref, inner_ref, outer_ref, near_ref, first_ref, second_ref, shift_ref, done_ref,
     out_ref, taps_ref, sum_ref,
 ):
     lane = iota((ROWS, 128), 1)
-    place = place_ref[0]
-    before = jnp.where(place == 0, 0.0, before_ref[...].astype(F32))
-    after = jnp.where(place == place_ref[1] - 1, 0.0, after_ref[...].astype(F32))
+    place, places = lax.axis_index("rng"), lax.axis_size("rng")
+    odd = place % 2 == 1
+    inner, outer = inner_ref[...].astype(F32), outer_ref[...].astype(F32)
+    before = jnp.where(place == 0, 0.0, jnp.where(odd, inner, outer))
+    after = jnp.where(place == places - 1, 0.0, jnp.where(odd, outer, inner))
 
     def pixels(slot, part):
         k = 2 * slot + part
@@ -272,7 +275,7 @@
         spot = iota((rows, 512), 1)
         column = spot % 32 + jnp.where(spot % 64 < 32, -4, 232)
         low = jnp.where(place == 0, 0, -128)
-        high = jnp.where(place == place_ref[1] - 1, COLS, 2 * COLS)
+        high = jnp.where(place == places - 1, COLS, 2 * COLS)
         return (column >= low) & (column < high)
 
     valid = in_frame(24)
@@ -386,7 +389,7 @@
         cost_estimate=pl.CostEstimate(flops=10**7, bytes_accessed=10**6, transcendentals=0),
     )(first, second, latter_filter_shift)
 
-    pixels, first_edge, last_edge = pl.pallas_call(
+    pixels, to_inner, to_outer = pl.pallas_call(
         pick_kernel,
         out_shape=(
             jax.ShapeDtypeStruct((3, 2, ROWS, COLS), BF16),
@@ -398,10 +401,9 @@
         compiler_params=small(8),
     )(picks, bands)
 
-    up = [(i, (i + 1) % rng_count) for i in range(rng_count)]
-    down = [(j, i) for i, j in up]
-    before = lax.ppermute(last_edge, "rng", up)
-    after = lax.ppermute(first_edge, "rng", down)
+    inner = lax.ppermute(to_inner, "rng", [(i, i ^ 1) for i in range(rng_count)])
+    partner = [i if i in (0, rng_count - 1) else ((i + 1) ^ 1) - 1 for i in range(rng_count)]
+    outer = lax.ppermute(to_outer, "rng", list(enumerate(partner)))
 
     middle = pl.pallas_call(
         middle_kernel,
@@ -416,18 +418,17 @@
         cost_estimate=pl.CostEstimate(flops=4 * 10**9, bytes_accessed=10**7, transcendentals=10**5),
     )(pixels, near, first_spread, second_spread, shift)
 
-    place = jnp.stack([lax.axis_index("rng"), jnp.int32(rng_count)]).astype(jnp.int32)
     return pl.pallas_call(
         edge_kernel,
         out_shape=jax.ShapeDtypeStruct((2, 2, ROWS, COLS), F32),
-        in_specs=[smem()] + [vmem()] * 8,
+        in_specs=[vmem()] * 8,
         out_specs=vmem(),
         scratch_shapes=[
             pltpu.VMEM((3, 256, 512), BF16),
             pltpu.VMEM((2, 88, 512), F32),
         ],
         compiler_params=small(16),
-    )(place, pixels, before, after, near, first_spread, second_spread, shift, middle)
+    )(pixels, inner, outer, near, first_spread, second_spread, shift, middle)
 
 
 def solution(mesh):

time: 33.1 us -> 31.5 us (0.952)
  the two profiles are of different devices: /device:TPU:1 before, /device:TPU:128 now
where the time goes in v4:
time: 31.5 us; the launch traced here: 31.1 us
  starting transfers between devices  10.6 us (34%)
  Pallas kernels  7.52 us (24%)
  waiting for transfers between devices  7.18 us (23%)
  local copies, waits for them, and re-layouts  4.37 us (14%)
  between operations  0.83 us (3%)
  other arithmetic  0.57 us (2%)
    all_to_all x1, starting transfers between devices, local(): lax.all_to_all(sent, 'date', split_axis=0, concat_axis=0, tiled=True)  7.03 us
    all_to_all x1, waiting for transfers between devices, local(): lax.all_to_all(sent, 'date', split_axis=0, concat_axis=0, tiled=True)  5.14 us
    unnamed x14, local copies, waits for them, and re-layouts  4.07 us
    pallas_call x1, Pallas kernels, local(): pl.pallas_call(middle_kernel, out_shape=jax.ShapeDtypeStruct((2, 2, ROWS,...  2.88 us
    ppermute x1, starting transfers between devices, local(): outer = lax.ppermute(to_outer, 'rng', list(enumerate(partner)))  2.79 us
    pallas_call x1, Pallas kernels, local(): pl.pallas_call(edge_kernel, out_shape=jax.ShapeDtypeStruct((2, 2, ROWS, C...  2.28 us
    ppermute x1, waiting for transfers between devices, local(): outer = lax.ppermute(to_outer, 'rng', list(enumerate(partner)))  2.04 us
    pallas_call x1, Pallas kernels, local(): pl.pallas_call(spread_kernel, out_shape=(jax.ShapeDtypeStruct((2 * WIDE,...  1.32 us
  transfers between devices with their start and end apart: 3, of which 2 were waited for; matrix products, arithmetic and copies ran while one was open for 3% of the time, Pallas kernels for 14%

profile of v4, /device:TPU:128, one launch (start us, length us, event | category | flops | bytes accessed | tf_op | source)
XLA Modules:
  0.0 31.1 jit_solution(3160513937134589409)
XLA Ops:
  0.0 0.0 copy-start
  0.7 0.0 copy-start.1
  0.7 0.9 %copy-done.1 = bf16[32,2,8,256]{3,2,1,0:T(8,128)(2,1)S(1)} copy-done((bf16[32,2,8,256]{3,2,1,0:T(8,128)(2,1)S(1)}, bf16[32,2,8,256]{3,2,1,0:T(8,128)(2,1)}, u32[]{:S(2)}) %copy-start.1) | copy-done | bytes 262168
  1.6 0.8 %shard_map.82 = bf16[16,3,2,8,256]{4,3,2,1,0:T(8,128)(2,1)} custom-call(s32[1]{0:T(128)} %copy.13.chosen_ref, bf16[16,2,2,8,256]{4,3,2,1,0:T(8,128)(2,1)S(1)} %bitcast.12), custom_call_target="tpu_custom_call" | custom-call | tf_op jit(solution)/shard_map/pallas_call | solution.py:340
  2.4 7.0 %all-to-all-start = ((bf16[16,3,2,8,256]{4,3,2,1,0:T(8,128)(2,1)}), bf16[16,3,2,8,256]{4,3,2,1,0:T(8,128)(2,1)S(1)}, u32[]{:S(2)}, u32[]{:S(2)}) async-start(bf16[16,3,2,8,256]{4,3,2,1,0:T(8,128)(2,1)} %shard_map.82), calls=%async_computation | async-start | bytes 786432 | tf_op jit(solution)/shard_map/all_to_all | solution.py:347
  9.4 0.0 copy-start.3
  9.5 0.0 copy-done
  9.5 0.7 %copy-done.3 = f32[32,5,3,3]{0,3,2,1:T(4,128)S(1)} copy-done((f32[32,5,3,3]{0,3,2,1:T(4,128)S(1)}, f32[32,5,3,3]{0,3,2,1:T(4,128)}, u32[]{:S(2)}) %copy-start.3) | copy-done | bytes 5784
  10.2 0.1 copy.11
  10.3 0.0 copy-start.5
  10.3 0.7 %copy-done.5 = f32[32]{0:T(128)S(1)} copy-done((f32[32]{0:T(128)S(1)}, f32[32]{0:T(128)}, u32[]{:S(2)}) %copy-start.5) | copy-done | bytes 152
  10.9 0.0 copy-start.6
  10.9 0.1 copy.12
  11.0 0.6 %copy-done.6 = s32[64]{0:T(128)S(1)} copy-done((s32[64]{0:T(128)S(1)}, s32[64]{0:T(128)}, u32[]{:S(2)}) %copy-start.6) | copy-done | bytes 280
  11.6 0.2 select_reduce_fusion
  11.8 0.1 pad.7.clone
  11.9 0.1 fusion.3
  12.0 0.0 copy-start.4
  12.0 0.1 maximum_maximum_fusion.first_ref
  12.1 0.6 %copy-done.4 = f32[2,32,3,3]{1,0,3,2:T(2,128)S(1)} copy-done((f32[2,32,3,3]{1,0,3,2:T(2,128)S(1)}, f32[2,32,3,3]{1,0,3,2:T(2,128)}, u32[]{:S(2)}) %copy-start.4) | copy-done | bytes 2328
  12.7 0.0 copy-start.2
  12.7 0.6 %copy-done.2 = f32[2]{0:T(128)S(1)} copy-done((f32[2]{0:T(128)S(1)}, f32[2]{0:T(128)}, u32[]{:S(2)}) %copy-start.2) | copy-done | bytes 32
  13.4 1.3 %shard_map.84 = (bf16[384,256]{1,0:T(8,128)(2,1)S(1)}, bf16[96,192]{1,0:T(8,128)(2,1)S(1)}, f32[2,8,128]{2,1,0:T(8,128)S(1)}) custom-call(f32[32,48]{1,0:T(8,128)S(1)} %maximum_maximum_fusion.first_ref, f32[24,32]{1,0:T(8,128)S(1)} %pad.4.second_ref, f32[2]{0:T(128)S(1)} %copy-done.2), custom_call_target="tpu_custom_call" | custom-call | flops 10000000 | bytes 1000000 | tf_op jit(solution)/shard_map/pallas_call | solution.py:379
  14.7 0.1 add_convert_fusion.near_ref
  14.8 0.1 fusion.chosen_ref
  14.9 5.1 %all-to-all-done.bands_ref = bf16[16,3,2,8,256]{4,3,2,1,0:T(8,128)(2,1)S(1)} async-done(((bf16[16,3,2,8,256]{4,3,2,1,0:T(8,128)(2,1)}), bf16[16,3,2,8,256]{4,3,2,1,0:T(8,128)(2,1)S(1)}, u32[]{:S(2)}, u32[]{:S(2)}) %all-to-all-start) | async-done | bytes 393248 | tf_op jit(solution)/shard_map/all_to_all | solution.py:347
  20.0 0.3 shard_map.83
  20.3 0.8 %collective-permute-start = (bf16[64,128]{1,0:T(8,128)(2,1)S(1)}, bf16[64,128]{1,0:T(8,128)(2,1)S(1)}, u32[]{:S(2)}, u32[]{:S(2)}) collective-permute-start(bf16[64,128]{1,0:T(8,128)(2,1)S(1)} %get-tuple-element.12), channel_id=1, source_target_pairs={{0,1},{1,0},{2,3},{3,2},{4,5},{5,4},{6,7},{7,6},{8,9},{9,8},{10,11... | collective-permute-start | bytes 49160 | tf_op jit(solution)/shard_map/ppermute | solution.py:404
  21.0 2.8 %collective-permute-start.1 = (bf16[64,128]{1,0:T(8,128)(2,1)S(1)}, bf16[64,128]{1,0:T(8,128)(2,1)S(1)}, u32[]{:S(2)}, u32[]{:S(2)}) collective-permute-start(bf16[64,128]{1,0:T(8,128)(2,1)S(1)} %get-tuple-element.13), channel_id=1, source_target_pairs={{0,0},{1,2},{2,1},{3,4},{4,3},{5,6},{6,5},{7,8},{8,7},{9,10},{10,9... | collective-permute-start | bytes 49160 | tf_op jit(solution)/shard_map/ppermute | solution.py:406
  23.8 2.9 %shard_map.85.done_ref = f32[2,2,64,256]{3,2,1,0:T(8,128)S(1)} custom-call(bf16[3,2,64,256]{3,2,1,0:T(8,128)(2,1)S(1)} %get-tuple-element.11.window_ref, bf16[96,128]{1,0:T(8,128)(2,1)S(1)} %add_convert_fusion.near_ref, bf16[384,256]{1,0:T(8,128)(2,1)S(1)} %get-tuple-element.14.first_ref, bf16[96,192]{1,0:T(8,128)(2,1)S(1)} %get-tuple-element.15.second_ref, ...), custom_call_target="tpu_custom_call" | custom-call | flops 4000000000 | bytes 10000000 | tf_op jit(solution)/shard_map/pallas_call | solution.py:408
  26.7 0.0 collective-permute-done.inner_ref
  26.7 2.0 %collective-permute-done.1.outer_ref = bf16[64,128]{1,0:T(8,128)(2,1)S(1)} collective-permute-done((bf16[64,128]{1,0:T(8,128)(2,1)S(1)}, bf16[64,128]{1,0:T(8,128)(2,1)S(1)}, u32[]{:S(2)}, u32[]{:S(2)}) %collective-permute-start.1) | collective-permute-done | bytes 16416 | tf_op jit(solution)/shard_map/ppermute | solution.py:406
  28.8 2.3 %shard_map.86 = f32[2,2,64,256]{3,2,1,0:T(8,128)} custom-call(bf16[3,2,64,256]{3,2,1,0:T(8,128)(2,1)S(1)} %get-tuple-element.11.window_ref, bf16[64,128]{1,0:T(8,128)(2,1)S(1)} %collective-permute-done.inner_ref, bf16[64,128]{1,0:T(8,128)(2,1)S(1)} %collective-permute-done.1.outer_ref, bf16[96,128]{1,0:T(8,128)(2,1)S(1)} %add_convert_fusion.near_ref, ...), custom_call_target="tpu_custom_call" | custom-call | tf_op jit(solution)/shard_map/pallas_call | solution.py:421
  (9 shorter events, 0.1 us)
Async XLA Ops:
  0.0 9.5 %copy-start = (s32[32,1,64]{2,1,0:T(1,128)S(1)}, s32[32,1,64]{2,1,0:T(1,128)}, u32[]{:S(2)}) copy-start(s32[32,1,64]{2,1,0:T(1,128)} %param.9) | copy-start | bytes 24580
  0.7 1.0 %copy-start.1 = (bf16[32,2,8,256]{3,2,1,0:T(8,128)(2,1)S(1)}, bf16[32,2,8,256]{3,2,1,0:T(8,128)(2,1)}, u32[]{:S(2)}) copy-start(bf16[32,2,8,256]{3,2,1,0:T(8,128)(2,1)} %param.8) | copy-start | bytes 786436
  2.4 17.6 %all-to-all-start = ((bf16[16,3,2,8,256]{4,3,2,1,0:T(8,128)(2,1)}), bf16[16,3,2,8,256]{4,3,2,1,0:T(8,128)(2,1)S(1)}, u32[]{:S(2)}, u32[]{:S(2)}) async-start(bf16[16,3,2,8,256]{4,3,2,1,0:T(8,128)(2,1)} %shard_map.82), calls=%async_computation | async-start | bytes 786432 | tf_op jit(solution)/shard_map/all_to_all | solution.py:347
  9.4 0.8 %copy-start.3 = (f32[32,5,3,3]{0,3,2,1:T(4,128)S(1)}, f32[32,5,3,3]{0,3,2,1:T(4,128)}, u32[]{:S(2)}) copy-start(f32[32,5,3,3]{0,3,2,1:T(4,128)} %param.12) | copy-start | bytes 17284
  10.3 0.7 %copy-start.5 = (f32[32]{0:T(128)S(1)}, f32[32]{0:T(128)}, u32[]{:S(2)}) copy-start(f32[32]{0:T(128)} %param.13) | copy-start | bytes 388
  10.9 0.7 %copy-start.6 = (s32[64]{0:T(128)S(1)}, s32[64]{0:T(128)}, u32[]{:S(2)}) copy-start(s32[64]{0:T(128)} %param.11) | copy-start | bytes 772
  12.0 0.7 %copy-start.4 = (f32[2,32,3,3]{1,0,3,2:T(2,128)S(1)}, f32[2,32,3,3]{1,0,3,2:T(2,128)}, u32[]{:S(2)}) copy-start(f32[2,32,3,3]{1,0,3,2:T(2,128)} %param.14) | copy-start | bytes 6916
  12.7 0.7 %copy-start.2 = (f32[2]{0:T(128)S(1)}, f32[2]{0:T(128)}, u32[]{:S(2)}) copy-start(f32[2]{0:T(128)} %shift_ref.1) | copy-start | bytes 28
  20.3 6.4 %collective-permute-start = (bf16[64,128]{1,0:T(8,128)(2,1)S(1)}, bf16[64,128]{1,0:T(8,128)(2,1)S(1)}, u32[]{:S(2)}, u32[]{:S(2)}) collective-permute-start(bf16[64,128]{1,0:T(8,128)(2,1)S(1)} %get-tuple-element.12), channel_id=1, source_target_pairs={{0,1},{1,0},{2,3},{3,2},{4,5},{5,4},{6,7},{7,6},{8,9},{9,8},{10,11... | collective-permute-start | bytes 49160 | tf_op jit(solution)/shard_map/ppermute | solution.py:404
  21.0 7.7 %collective-permute-start.1 = (bf16[64,128]{1,0:T(8,128)(2,1)S(1)}, bf16[64,128]{1,0:T(8,128)(2,1)S(1)}, u32[]{:S(2)}, u32[]{:S(2)}) collective-permute-start(bf16[64,128]{1,0:T(8,128)(2,1)S(1)} %get-tuple-element.13), channel_id=1, source_target_pairs={{0,0},{1,2},{2,1},{3,4},{4,3},{5,6},{6,5},{7,8},{8,7},{9,10},{10,9... | collective-permute-start | bytes 49160 | tf_op jit(solution)/shard_map/ppermute | solution.py:406

commit v5 on v4

--- a/solution.py
+++ b/solution.py
@@ -402,8 +402,12 @@
     )(picks, bands)
 
     inner = lax.ppermute(to_inner, "rng", [(i, i ^ 1) for i in range(rng_count)])
-    partner = [i if i in (0, rng_count - 1) else ((i + 1) ^ 1) - 1 for i in range(rng_count)]
-    outer = lax.ppermute(to_outer, "rng", list(enumerate(partner)))
+    swaps = []
+    for d in range(lax.axis_size("date")):
+        for i in range(rng_count):
+            across = (d ^ 1, i) if i in (0, rng_count - 1) else (d, ((i + 1) ^ 1) - 1)
+            swaps.append((d * rng_count + i, across[0] * rng_count + across[1]))
+    outer = lax.ppermute(to_outer, ("date", "rng"), swaps)
 
     middle = pl.pallas_call(
         middle_kernel,

time: 31.5 us -> 29.6 us (0.940)
  starting transfers between devices: 10.6 us -> 8.69 us
    ppermute x1, starting transfers between devices: 2.79 us -> 0.89 us  [local(): outer = lax.ppermute(to_outer, ('date', 'rng'), swaps)]
where the time goes in v5:
time: 29.6 us; the launch traced here: 29.2 us
  starting transfers between devices  8.69 us (29%)
  Pallas kernels  7.52 us (25%)
  waiting for transfers between devices  7.2 us (24%)
  local copies, waits for them, and re-layouts  4.37 us (15%)
  between operations  0.83 us (3%)
  other arithmetic  0.57 us (2%)
    all_to_all x1, starting transfers between devices, local(): lax.all_to_all(sent, 'date', split_axis=0, concat_axis=0, tiled=True)  7.03 us
    all_to_all x1, waiting for transfers between devices, local(): lax.all_to_all(sent, 'date', split_axis=0, concat_axis=0, tiled=True)  5.14 us
    unnamed x14, local copies, waits for them, and re-layouts  4.07 us
    pallas_call x1, Pallas kernels, local(): pl.pallas_call(middle_kernel, out_shape=jax.ShapeDtypeStruct((2, 2, ROWS,...  2.88 us
    pallas_call x1, Pallas kernels, local(): pl.pallas_call(edge_kernel, out_shape=jax.ShapeDtypeStruct((2, 2, ROWS, C...  2.28 us
    ppermute x1, waiting for transfers between devices, local(): outer = lax.ppermute(to_outer, ('date', 'rng'), swaps)  2.06 us
    pallas_call x1, Pallas kernels, local(): pl.pallas_call(spread_kernel, out_shape=(jax.ShapeDtypeStruct((2 * WIDE,...  1.32 us
    ppermute x1, starting transfers between devices, local(): outer = lax.ppermute(to_outer, ('date', 'rng'), swaps)  0.89 us
  transfers between devices with their start and end apart: 3, of which 2 were waited for; matrix products, arithmetic and copies ran while one was open for 3% of the time, Pallas kernels for 14%

profile of v5, /device:TPU:128, one launch (start us, length us, event | category | flops | bytes accessed | tf_op | source)
XLA Modules:
  0.0 29.2 jit_solution(10952111342717739985)
XLA Ops:
  0.0 0.0 copy-start
  0.7 0.0 copy-start.1
  0.7 0.9 %copy-done.1 = bf16[32,2,8,256]{3,2,1,0:T(8,128)(2,1)S(1)} copy-done((bf16[32,2,8,256]{3,2,1,0:T(8,128)(2,1)S(1)}, bf16[32,2,8,256]{3,2,1,0:T(8,128)(2,1)}, u32[]{:S(2)}) %copy-start.1) | copy-done | bytes 262168
  1.6 0.8 %shard_map.82 = bf16[16,3,2,8,256]{4,3,2,1,0:T(8,128)(2,1)} custom-call(s32[1]{0:T(128)} %copy.13.chosen_ref, bf16[16,2,2,8,256]{4,3,2,1,0:T(8,128)(2,1)S(1)} %bitcast.12), custom_call_target="tpu_custom_call" | custom-call | tf_op jit(solution)/shard_map/pallas_call | solution.py:340
  2.4 7.0 %all-to-all-start = ((bf16[16,3,2,8,256]{4,3,2,1,0:T(8,128)(2,1)}), bf16[16,3,2,8,256]{4,3,2,1,0:T(8,128)(2,1)S(1)}, u32[]{:S(2)}, u32[]{:S(2)}) async-start(bf16[16,3,2,8,256]{4,3,2,1,0:T(8,128)(2,1)} %shard_map.82), calls=%async_computation | async-start | bytes 786432 | tf_op jit(solution)/shard_map/all_to_all | solution.py:347
  9.4 0.0 copy-start.3
  9.5 0.0 copy-done
  9.5 0.7 %copy-done.3 = f32[32,5,3,3]{0,3,2,1:T(4,128)S(1)} copy-done((f32[32,5,3,3]{0,3,2,1:T(4,128)S(1)}, f32[32,5,3,3]{0,3,2,1:T(4,128)}, u32[]{:S(2)}) %copy-start.3) | copy-done | bytes 5784
  10.2 0.1 copy.11
  10.3 0.0 copy-start.5
  10.3 0.7 %copy-done.5 = f32[32]{0:T(128)S(1)} copy-done((f32[32]{0:T(128)S(1)}, f32[32]{0:T(128)}, u32[]{:S(2)}) %copy-start.5) | copy-done | bytes 152
  10.9 0.0 copy-start.6
  10.9 0.1 copy.12
  11.0 0.6 %copy-done.6 = s32[64]{0:T(128)S(1)} copy-done((s32[64]{0:T(128)S(1)}, s32[64]{0:T(128)}, u32[]{:S(2)}) %copy-start.6) | copy-done | bytes 280
  11.6 0.2 select_reduce_fusion
  11.8 0.1 pad.7.clone
  11.9 0.1 fusion.3
  12.0 0.0 copy-start.4
  12.0 0.1 maximum_maximum_fusion.first_ref
  12.1 0.6 %copy-done.4 = f32[2,32,3,3]{1,0,3,2:T(2,128)S(1)} copy-done((f32[2,32,3,3]{1,0,3,2:T(2,128)S(1)}, f32[2,32,3,3]{1,0,3,2:T(2,128)}, u32[]{:S(2)}) %copy-start.4) | copy-done | bytes 2328
  12.7 0.0 copy-start.2
  12.7 0.6 %copy-done.2 = f32[2]{0:T(128)S(1)} copy-done((f32[2]{0:T(128)S(1)}, f32[2]{0:T(128)}, u32[]{:S(2)}) %copy-start.2) | copy-done | bytes 32
  13.4 1.3 %shard_map.84 = (bf16[384,256]{1,0:T(8,128)(2,1)S(1)}, bf16[96,192]{1,0:T(8,128)(2,1)S(1)}, f32[2,8,128]{2,1,0:T(8,128)S(1)}) custom-call(f32[32,48]{1,0:T(8,128)S(1)} %maximum_maximum_fusion.first_ref, f32[24,32]{1,0:T(8,128)S(1)} %pad.4.second_ref, f32[2]{0:T(128)S(1)} %copy-done.2), custom_call_target="tpu_custom_call" | custom-call | flops 10000000 | bytes 1000000 | tf_op jit(solution)/shard_map/pallas_call | solution.py:379
  14.7 0.1 add_convert_fusion.near_ref
  14.8 0.1 fusion.chosen_ref
  14.9 5.1 %all-to-all-done.bands_ref = bf16[16,3,2,8,256]{4,3,2,1,0:T(8,128)(2,1)S(1)} async-done(((bf16[16,3,2,8,256]{4,3,2,1,0:T(8,128)(2,1)}), bf16[16,3,2,8,256]{4,3,2,1,0:T(8,128)(2,1)S(1)}, u32[]{:S(2)}, u32[]{:S(2)}) %all-to-all-start) | async-done | bytes 393248 | tf_op jit(solution)/shard_map/all_to_all | solution.py:347
  20.0 0.3 shard_map.83
  20.3 0.8 %collective-permute-start = (bf16[64,128]{1,0:T(8,128)(2,1)S(1)}, bf16[64,128]{1,0:T(8,128)(2,1)S(1)}, u32[]{:S(2)}, u32[]{:S(2)}) collective-permute-start(bf16[64,128]{1,0:T(8,128)(2,1)S(1)} %get-tuple-element.12), channel_id=1, source_target_pairs={{0,1},{1,0},{2,3},{3,2},{4,5},{5,4},{6,7},{7,6},{8,9},{9,8},{10,11... | collective-permute-start | bytes 49160 | tf_op jit(solution)/shard_map/ppermute | solution.py:404
  21.0 0.9 %collective-permute-start.1 = (bf16[64,128]{1,0:T(8,128)(2,1)S(1)}, bf16[64,128]{1,0:T(8,128)(2,1)S(1)}, u32[]{:S(2)}, u32[]{:S(2)}) collective-permute-start(bf16[64,128]{1,0:T(8,128)(2,1)S(1)} %get-tuple-element.13), channel_id=1, source_target_pairs={{0,16},{1,2},{2,1},{3,4},{4,3},{5,6},{6,5},{7,8},{8,7},{9,10},{10,... | collective-permute-start | bytes 49160 | tf_op jit(solution)/shard_map/ppermute | solution.py:410
  21.9 2.9 %shard_map.85.done_ref = f32[2,2,64,256]{3,2,1,0:T(8,128)S(1)} custom-call(bf16[3,2,64,256]{3,2,1,0:T(8,128)(2,1)S(1)} %get-tuple-element.11.window_ref, bf16[96,128]{1,0:T(8,128)(2,1)S(1)} %add_convert_fusion.near_ref, bf16[384,256]{1,0:T(8,128)(2,1)S(1)} %get-tuple-element.14.first_ref, bf16[96,192]{1,0:T(8,128)(2,1)S(1)} %get-tuple-element.15.second_ref, ...), custom_call_target="tpu_custom_call" | custom-call | flops 4000000000 | bytes 10000000 | tf_op jit(solution)/shard_map/pallas_call | solution.py:412
  24.8 0.0 collective-permute-done.inner_ref
  24.8 2.1 %collective-permute-done.1.outer_ref = bf16[64,128]{1,0:T(8,128)(2,1)S(1)} collective-permute-done((bf16[64,128]{1,0:T(8,128)(2,1)S(1)}, bf16[64,128]{1,0:T(8,128)(2,1)S(1)}, u32[]{:S(2)}, u32[]{:S(2)}) %collective-permute-start.1) | collective-permute-done | bytes 16416 | tf_op jit(solution)/shard_map/ppermute | solution.py:410
  26.9 2.3 %shard_map.86 = f32[2,2,64,256]{3,2,1,0:T(8,128)} custom-call(bf16[3,2,64,256]{3,2,1,0:T(8,128)(2,1)S(1)} %get-tuple-element.11.window_ref, bf16[64,128]{1,0:T(8,128)(2,1)S(1)} %collective-permute-done.inner_ref, bf16[64,128]{1,0:T(8,128)(2,1)S(1)} %collective-permute-done.1.outer_ref, bf16[96,128]{1,0:T(8,128)(2,1)S(1)} %add_convert_fusion.near_ref, ...), custom_call_target="tpu_custom_call" | custom-call | tf_op jit(solution)/shard_map/pallas_call | solution.py:425
  (9 shorter events, 0.1 us)
Async XLA Ops:
  0.0 9.5 %copy-start = (s32[32,1,64]{2,1,0:T(1,128)S(1)}, s32[32,1,64]{2,1,0:T(1,128)}, u32[]{:S(2)}) copy-start(s32[32,1,64]{2,1,0:T(1,128)} %param.9) | copy-start | bytes 24580
  0.7 1.0 %copy-start.1 = (bf16[32,2,8,256]{3,2,1,0:T(8,128)(2,1)S(1)}, bf16[32,2,8,256]{3,2,1,0:T(8,128)(2,1)}, u32[]{:S(2)}) copy-start(bf16[32,2,8,256]{3,2,1,0:T(8,128)(2,1)} %param.8) | copy-start | bytes 786436
  2.4 17.6 %all-to-all-start = ((bf16[16,3,2,8,256]{4,3,2,1,0:T(8,128)(2,1)}), bf16[16,3,2,8,256]{4,3,2,1,0:T(8,128)(2,1)S(1)}, u32[]{:S(2)}, u32[]{:S(2)}) async-start(bf16[16,3,2,8,256]{4,3,2,1,0:T(8,128)(2,1)} %shard_map.82), calls=%async_computation | async-start | bytes 786432 | tf_op jit(solution)/shard_map/all_to_all | solution.py:347
  9.4 0.8 %copy-start.3 = (f32[32,5,3,3]{0,3,2,1:T(4,128)S(1)}, f32[32,5,3,3]{0,3,2,1:T(4,128)}, u32[]{:S(2)}) copy-start(f32[32,5,3,3]{0,3,2,1:T(4,128)} %param.12) | copy-start | bytes 17284
  10.3 0.7 %copy-start.5 = (f32[32]{0:T(128)S(1)}, f32[32]{0:T(128)}, u32[]{:S(2)}) copy-start(f32[32]{0:T(128)} %param.13) | copy-start | bytes 388
  10.9 0.7 %copy-start.6 = (s32[64]{0:T(128)S(1)}, s32[64]{0:T(128)}, u32[]{:S(2)}) copy-start(s32[64]{0:T(128)} %param.11) | copy-start | bytes 772
  12.0 0.7 %copy-start.4 = (f32[2,32,3,3]{1,0,3,2:T(2,128)S(1)}, f32[2,32,3,3]{1,0,3,2:T(2,128)}, u32[]{:S(2)}) copy-start(f32[2,32,3,3]{1,0,3,2:T(2,128)} %param.14) | copy-start | bytes 6916
  12.7 0.7 %copy-start.2 = (f32[2]{0:T(128)S(1)}, f32[2]{0:T(128)}, u32[]{:S(2)}) copy-start(f32[2]{0:T(128)} %shift_ref.1) | copy-start | bytes 28
  20.3 4.5 %collective-permute-start = (bf16[64,128]{1,0:T(8,128)(2,1)S(1)}, bf16[64,128]{1,0:T(8,128)(2,1)S(1)}, u32[]{:S(2)}, u32[]{:S(2)}) collective-permute-start(bf16[64,128]{1,0:T(8,128)(2,1)S(1)} %get-tuple-element.12), channel_id=1, source_target_pairs={{0,1},{1,0},{2,3},{3,2},{4,5},{5,4},{6,7},{7,6},{8,9},{9,8},{10,11... | collective-permute-start | bytes 49160 | tf_op jit(solution)/shard_map/ppermute | solution.py:404
  21.0 5.8 %collective-permute-start.1 = (bf16[64,128]{1,0:T(8,128)(2,1)S(1)}, bf16[64,128]{1,0:T(8,128)(2,1)S(1)}, u32[]{:S(2)}, u32[]{:S(2)}) collective-permute-start(bf16[64,128]{1,0:T(8,128)(2,1)S(1)} %get-tuple-element.13), channel_id=1, source_target_pairs={{0,16},{1,2},{2,1},{3,4},{4,3},{5,6},{6,5},{7,8},{8,7},{9,10},{10,... | collective-permute-start | bytes 49160 | tf_op jit(solution)/shard_map/ppermute | solution.py:410

commit v6 on v5

--- a/solution.py
+++ b/solution.py
@@ -42,7 +42,17 @@
         sent_ref[band, 2] = master
 
 
-def spread_kernel(first_ref, second_ref, shift_ref, first_out, second_out, shift_out):
+def spread_kernel(first_ref, second_ref, shift_ref, first_out, second_out, shift_out, band_out, edge_out):
+    gap = iota((COLS, COLS), 0) - iota((COLS, COLS), 1) + BOX_RG // 2
+    band_out[...] = ((gap >= 0) & (gap < BOX_RG)).astype(BF16)
+    source, target = iota((128, 128), 0), iota((128, 128), 1)
+    from_col = jnp.where(source < 64, source - 16, source + 160)
+    side = target % 64 // 32
+    to_col = target % 32 + jnp.where(side == 0, -4, 232)
+    gap = from_col - to_col + BOX_RG // 2
+    near = (gap >= 0) & (gap < BOX_RG) & (source // 64 == side)
+    for d in range(2):
+        edge_out[d] = (near & (target // 64 == d)).astype(BF16)
     row, col = iota((WIDE, 128), 0), iota((WIDE, 128), 1)
     tap = col % 8 - row // HIDDEN
     widen = (iota((WIDE, HIDDEN), 0) % HIDDEN == iota((WIDE, HIDDEN), 1)).astype(BF16)
@@ -189,11 +199,10 @@
     return window + jnp.where(row < 2, pltpu.roll(previous, 2, 0), 0.0)
 
 
-def middle_kernel(window_ref, near_ref, first_ref, second_ref, shift_ref, out_ref, taps_ref, sum_ref):
+def middle_kernel(window_ref, near_ref, first_ref, second_ref, shift_ref, band_ref, out_ref, taps_ref, sum_ref):
     re = [window_ref[s, 0].astype(F32) for s in range(3)]
     im = [window_ref[s, 1].astype(F32) for s in range(3)]
-    gap = iota((COLS, COLS), 0) - iota((COLS, COLS), 1) + BOX_RG // 2
-    band = ((gap >= 0) & (gap < BOX_RG)).astype(BF16)
+    band = band_ref[...]
     planes = jnp.concatenate(products(re, im), axis=0)
     summed = matmul(jnp.concatenate(halves(planes), axis=1), jnp.concatenate([band, band], axis=0))
     live = 8 * BLOCKS
@@ -232,7 +241,7 @@
 
 
 def edge_kernel(
-    window_ref, inner_ref, outer_ref, near_ref, first_ref, second_ref, shift_ref, done_ref,
+    window_ref, inner_ref, outer_ref, near_ref, first_ref, second_ref, shift_ref, band_ref, done_ref,
     out_ref, taps_ref, sum_ref,
 ):
     lane = iota((ROWS, 128), 1)
@@ -255,13 +264,7 @@
         return jnp.where(lane < 112, tile, 0.0)
 
     planes = products([pixels(s, 0) for s in range(3)], [pixels(s, 1) for s in range(3)])
-    source, target = iota((128, 128), 0), iota((128, 128), 1)
-    from_col = jnp.where(source < 64, source - 16, source + 160)
-    side = target % 64 // 32
-    to_col = target % 32 + jnp.where(side == 0, -4, 232)
-    gap = from_col - to_col + BOX_RG // 2
-    near = (gap >= 0) & (gap < BOX_RG) & (source // 64 == side)
-    bands = [(near & (target // 64 == d)).astype(BF16) for d in range(2)]
+    bands = [band_ref[d] for d in range(2)]
     band = jnp.concatenate([bands[0], bands[0], bands[1], bands[1]], axis=0)
     dates = [jnp.concatenate([planes[0]] + planes[1 + 4 * d : 5 + 4 * d], axis=0) for d in range(2)]
     summed = matmul(jnp.concatenate(halves(dates[0]) + halves(dates[1]), axis=1), band)
@@ -376,15 +379,17 @@
     second = jnp.pad(
         jnp.transpose(latter_filter_kernel, (2, 3, 0, 1)).reshape(18, HIDDEN), ((0, 6), (0, 0))
     )
-    first_spread, second_spread, shift = pl.pallas_call(
+    first_spread, second_spread, shift, band, edge_band = pl.pallas_call(
         spread_kernel,
         out_shape=(
             jax.ShapeDtypeStruct((2 * WIDE, COLS), BF16),
             jax.ShapeDtypeStruct((96, WIDE), BF16),
             jax.ShapeDtypeStruct((2, 8, 128), F32),
+            jax.ShapeDtypeStruct((COLS, COLS), BF16),
+            jax.ShapeDtypeStruct((2, 128, 128), BF16),
         ),
         in_specs=[vmem()] * 2 + [smem()],
-        out_specs=(vmem(),) * 3,
+        out_specs=(vmem(),) * 5,
         compiler_params=small(8),
         cost_estimate=pl.CostEstimate(flops=10**7, bytes_accessed=10**6, transcendentals=0),
     )(first, second, latter_filter_shift)
@@ -412,7 +417,7 @@
     middle = pl.pallas_call(
         middle_kernel,
         out_shape=jax.ShapeDtypeStruct((2, 2, ROWS, COLS), F32),
-        in_specs=[vmem()] * 5,
+        in_specs=[vmem()] * 6,
         out_specs=vmem(),
         scratch_shapes=[
             pltpu.VMEM((BLOCKS, 256, 2 * COLS), BF16),
@@ -420,19 +425,19 @@
         ],
         compiler_params=small(16),
         cost_estimate=pl.CostEstimate(flops=4 * 10**9, bytes_accessed=10**7, transcendentals=10**5),
-    )(pixels, near, first_spread, second_spread, shift)
+    )(pixels, near, first_spread, second_spread, shift, band)
 
     return pl.pallas_call(
         edge_kernel,
         out_shape=jax.ShapeDtypeStruct((2, 2, ROWS, COLS), F32),
-        in_specs=[vmem()] * 8,
+        in_specs=[vmem()] * 9,
         out_specs=vmem(),
         scratch_shapes=[
             pltpu.VMEM((3, 256, 512), BF16),
             pltpu.VMEM((2, 88, 512), F32),
         ],
         compiler_params=small(16),
-    )(pixels, inner, outer, near, first_spread, second_spread, shift, middle)
+    )(pixels, inner, outer, near, first_spread, second_spread, shift, edge_band, middle)
 
 
 def solution(mesh):

time: 29.6 us -> 29.6 us (level)
  local copies, waits for them, and re-layouts: 4.37 us -> 3.71 us
  waiting for transfers between devices: 7.2 us -> 7.83 us
    unnamed x14, local copies, waits for them, and re-layouts: 4.07 us -> 3.42 us
    all_to_all x1, waiting for transfers between devices: 5.14 us -> 5.75 us  [local(): lax.all_to_all(sent, 'date', split_axis=0, concat_axis=0, tiled=True)]
where the time goes in v6:
time: 29.6 us; the launch traced here: 29.2 us
  starting transfers between devices  8.69 us (29%)
  waiting for transfers between devices  7.83 us (26%)
  Pallas kernels  7.55 us (26%)
  local copies, waits for them, and re-layouts  3.71 us (13%)
  between operations  0.84 us (3%)
  other arithmetic  0.57 us (2%)
    all_to_all x1, starting transfers between devices, local(): lax.all_to_all(sent, 'date', split_axis=0, concat_axis=0, tiled=True)  7.03 us
    all_to_all x1, waiting for transfers between devices, local(): lax.all_to_all(sent, 'date', split_axis=0, concat_axis=0, tiled=True)  5.75 us
    unnamed x14, local copies, waits for them, and re-layouts  3.42 us
    pallas_call x1, Pallas kernels, local(): pl.pallas_call(middle_kernel, out_shape=jax.ShapeDtypeStruct((2, 2, ROWS,...  2.87 us
    pallas_call x1, Pallas kernels, local(): pl.pallas_call(edge_kernel, out_shape=jax.ShapeDtypeStruct((2, 2, ROWS, C...  2.29 us
    ppermute x1, waiting for transfers between devices, local(): outer = lax.ppermute(to_outer, ('date', 'rng'), swaps)  2.07 us
    pallas_call x1, Pallas kernels, local(): pl.pallas_call(spread_kernel, out_shape=(jax.ShapeDtypeStruct((2 * WIDE,...  1.35 us
    ppermute x1, starting transfers between devices, local(): outer = lax.ppermute(to_outer, ('date', 'rng'), swaps)  0.89 us
  transfers between devices with their start and end apart: 3, of which 2 were waited for; matrix products, arithmetic and copies ran while one was open for 3% of the time, Pallas kernels for 14%

profile of v6, /device:TPU:128, one launch (start us, length us, event | category | flops | bytes accessed | tf_op | source)
XLA Modules:
  0.0 29.2 jit_solution(7624969301230997634)
XLA Ops:
  0.0 0.0 copy-start
  0.7 0.0 copy-start.1
  0.7 0.9 %copy-done.1 = bf16[32,2,8,256]{3,2,1,0:T(8,128)(2,1)S(1)} copy-done((bf16[32,2,8,256]{3,2,1,0:T(8,128)(2,1)S(1)}, bf16[32,2,8,256]{3,2,1,0:T(8,128)(2,1)}, u32[]{:S(2)}) %copy-start.1) | copy-done | bytes 262168
  1.6 0.8 %shard_map.82 = bf16[16,3,2,8,256]{4,3,2,1,0:T(8,128)(2,1)} custom-call(s32[1]{0:T(128)} %copy.13.chosen_ref, bf16[16,2,2,8,256]{4,3,2,1,0:T(8,128)(2,1)S(1)} %bitcast.12), custom_call_target="tpu_custom_call" | custom-call | tf_op jit(solution)/shard_map/pallas_call | solution.py:343
  2.4 7.0 %all-to-all-start = ((bf16[16,3,2,8,256]{4,3,2,1,0:T(8,128)(2,1)}), bf16[16,3,2,8,256]{4,3,2,1,0:T(8,128)(2,1)S(1)}, u32[]{:S(2)}, u32[]{:S(2)}) async-start(bf16[16,3,2,8,256]{4,3,2,1,0:T(8,128)(2,1)} %shard_map.82), calls=%async_computation | async-start | bytes 786432 | tf_op jit(solution)/shard_map/all_to_all | solution.py:350
  9.4 0.0 copy-start.3
  9.5 0.0 copy-done
  9.5 0.0 copy-start.5
  9.5 0.6 %copy-done.5 = f32[32]{0:T(128)S(1)} copy-done((f32[32]{0:T(128)S(1)}, f32[32]{0:T(128)}, u32[]{:S(2)}) %copy-start.5) | copy-done | bytes 152
  10.2 0.1 copy.12
  10.3 0.0 copy-done.3
  10.3 0.0 copy-start.6
  10.3 0.1 copy.11
  10.4 0.6 %copy-done.6 = s32[64]{0:T(128)S(1)} copy-done((s32[64]{0:T(128)S(1)}, s32[64]{0:T(128)}, u32[]{:S(2)}) %copy-start.6) | copy-done | bytes 280
  10.9 0.2 select_reduce_fusion
  11.1 0.1 pad.7.clone
  11.2 0.1 fusion.3
  11.3 0.0 copy-start.4
  11.3 0.1 maximum_maximum_fusion.first_ref
  11.4 0.6 %copy-done.4 = f32[2,32,3,3]{1,0,3,2:T(2,128)S(1)} copy-done((f32[2,32,3,3]{1,0,3,2:T(2,128)S(1)}, f32[2,32,3,3]{1,0,3,2:T(2,128)}, u32[]{:S(2)}) %copy-start.4) | copy-done | bytes 2328
  12.1 0.0 copy-start.2
  12.1 0.6 %copy-done.2 = f32[2]{0:T(128)S(1)} copy-done((f32[2]{0:T(128)S(1)}, f32[2]{0:T(128)}, u32[]{:S(2)}) %copy-start.2) | copy-done | bytes 32
  12.7 1.3 %shard_map.84 = (bf16[384,256]{1,0:T(8,128)(2,1)S(1)}, bf16[96,192]{1,0:T(8,128)(2,1)S(1)}, f32[2,8,128]{2,1,0:T(8,128)S(1)}, bf16[256,256]{1,0:T(8,128)(2,1)S(1)}, bf16[2,128,128]{2,1,0:T(8,128)(2,1)S(1)}) custom-call(f32[32,48]{1,0:T(8,128)S(1)} %maximum_maximum_fusion.first_ref, f32[24,32]{1,0:T(8,128)S(1)} %pad.4.second_ref, f32[2]{0:T(128)S(1)} %copy-done.2), custom_call_target="tpu_custom_call" | custom-call | flops 10000000 | bytes 1000000 | tf_op jit(solution)/shard_map/pallas_call | solution.py:382
  14.1 0.1 add_convert_fusion.near_ref
  14.2 0.1 fusion.chosen_ref
  14.3 5.8 %all-to-all-done.bands_ref = bf16[16,3,2,8,256]{4,3,2,1,0:T(8,128)(2,1)S(1)} async-done(((bf16[16,3,2,8,256]{4,3,2,1,0:T(8,128)(2,1)}), bf16[16,3,2,8,256]{4,3,2,1,0:T(8,128)(2,1)S(1)}, u32[]{:S(2)}, u32[]{:S(2)}) %all-to-all-start) | async-done | bytes 393248 | tf_op jit(solution)/shard_map/all_to_all | solution.py:350
  20.0 0.3 shard_map.83
  20.3 0.8 %collective-permute-start = (bf16[64,128]{1,0:T(8,128)(2,1)S(1)}, bf16[64,128]{1,0:T(8,128)(2,1)S(1)}, u32[]{:S(2)}, u32[]{:S(2)}) collective-permute-start(bf16[64,128]{1,0:T(8,128)(2,1)S(1)} %get-tuple-element.14), channel_id=1, source_target_pairs={{0,1},{1,0},{2,3},{3,2},{4,5},{5,4},{6,7},{7,6},{8,9},{9,8},{10,11... | collective-permute-start | bytes 49160 | tf_op jit(solution)/shard_map/ppermute | solution.py:409
  21.0 0.9 %collective-permute-start.1 = (bf16[64,128]{1,0:T(8,128)(2,1)S(1)}, bf16[64,128]{1,0:T(8,128)(2,1)S(1)}, u32[]{:S(2)}, u32[]{:S(2)}) collective-permute-start(bf16[64,128]{1,0:T(8,128)(2,1)S(1)} %get-tuple-element.15), channel_id=1, source_target_pairs={{0,16},{1,2},{2,1},{3,4},{4,3},{5,6},{6,5},{7,8},{8,7},{9,10},{10,... | collective-permute-start | bytes 49160 | tf_op jit(solution)/shard_map/ppermute | solution.py:415
  21.9 2.9 %shard_map.85.done_ref = f32[2,2,64,256]{3,2,1,0:T(8,128)S(1)} custom-call(bf16[3,2,64,256]{3,2,1,0:T(8,128)(2,1)S(1)} %get-tuple-element.13.window_ref, bf16[96,128]{1,0:T(8,128)(2,1)S(1)} %add_convert_fusion.near_ref, bf16[384,256]{1,0:T(8,128)(2,1)S(1)} %get-tuple-element.16.first_ref, bf16[96,192]{1,0:T(8,128)(2,1)S(1)} %get-tuple-element.17.second_ref, ...), custom_call_target="tpu_custom_call" | custom-call | flops 4000000000 | bytes 10000000 | tf_op jit(solution)/shard_map/pallas_call | solution.py:417
  24.8 0.0 collective-permute-done.inner_ref
  24.8 2.1 %collective-permute-done.1.outer_ref = bf16[64,128]{1,0:T(8,128)(2,1)S(1)} collective-permute-done((bf16[64,128]{1,0:T(8,128)(2,1)S(1)}, bf16[64,128]{1,0:T(8,128)(2,1)S(1)}, u32[]{:S(2)}, u32[]{:S(2)}) %collective-permute-start.1) | collective-permute-done | bytes 16416 | tf_op jit(solution)/shard_map/ppermute | solution.py:415
  26.9 2.3 %shard_map.86 = f32[2,2,64,256]{3,2,1,0:T(8,128)} custom-call(bf16[3,2,64,256]{3,2,1,0:T(8,128)(2,1)S(1)} %get-tuple-element.13.window_ref, bf16[64,128]{1,0:T(8,128)(2,1)S(1)} %collective-permute-done.inner_ref, bf16[64,128]{1,0:T(8,128)(2,1)S(1)} %collective-permute-done.1.outer_ref, bf16[96,128]{1,0:T(8,128)(2,1)S(1)} %add_convert_fusion.near_ref, ...), custom_call_target="tpu_custom_call" | custom-call | tf_op jit(solution)/shard_map/pallas_call | solution.py:430
  (9 shorter events, 0.1 us)
Async XLA Ops:
  0.0 9.5 %copy-start = (s32[32,1,64]{2,1,0:T(1,128)S(1)}, s32[32,1,64]{2,1,0:T(1,128)}, u32[]{:S(2)}) copy-start(s32[32,1,64]{2,1,0:T(1,128)} %param.9) | copy-start | bytes 24580
  0.7 1.0 %copy-start.1 = (bf16[32,2,8,256]{3,2,1,0:T(8,128)(2,1)S(1)}, bf16[32,2,8,256]{3,2,1,0:T(8,128)(2,1)}, u32[]{:S(2)}) copy-start(bf16[32,2,8,256]{3,2,1,0:T(8,128)(2,1)} %param.8) | copy-start | bytes 786436
  2.4 17.6 %all-to-all-start = ((bf16[16,3,2,8,256]{4,3,2,1,0:T(8,128)(2,1)}), bf16[16,3,2,8,256]{4,3,2,1,0:T(8,128)(2,1)S(1)}, u32[]{:S(2)}, u32[]{:S(2)}) async-start(bf16[16,3,2,8,256]{4,3,2,1,0:T(8,128)(2,1)} %shard_map.82), calls=%async_computation | async-start | bytes 786432 | tf_op jit(solution)/shard_map/all_to_all | solution.py:350
  9.4 0.8 %copy-start.3 = (f32[32,5,3,3]{0,3,2,1:T(4,128)S(1)}, f32[32,5,3,3]{0,3,2,1:T(4,128)}, u32[]{:S(2)}) copy-start(f32[32,5,3,3]{0,3,2,1:T(4,128)} %param.12) | copy-start | bytes 17284
  9.5 0.7 %copy-start.5 = (f32[32]{0:T(128)S(1)}, f32[32]{0:T(128)}, u32[]{:S(2)}) copy-start(f32[32]{0:T(128)} %param.13) | copy-start | bytes 388
  10.3 0.7 %copy-start.6 = (s32[64]{0:T(128)S(1)}, s32[64]{0:T(128)}, u32[]{:S(2)}) copy-start(s32[64]{0:T(128)} %param.11) | copy-start | bytes 772
  11.3 0.7 %copy-start.4 = (f32[2,32,3,3]{1,0,3,2:T(2,128)S(1)}, f32[2,32,3,3]{1,0,3,2:T(2,128)}, u32[]{:S(2)}) copy-start(f32[2,32,3,3]{1,0,3,2:T(2,128)} %param.14) | copy-start | bytes 6916
  12.1 0.7 %copy-start.2 = (f32[2]{0:T(128)S(1)}, f32[2]{0:T(128)}, u32[]{:S(2)}) copy-start(f32[2]{0:T(128)} %shift_ref.1) | copy-start | bytes 28
  20.3 4.5 %collective-permute-start = (bf16[64,128]{1,0:T(8,128)(2,1)S(1)}, bf16[64,128]{1,0:T(8,128)(2,1)S(1)}, u32[]{:S(2)}, u32[]{:S(2)}) collective-permute-start(bf16[64,128]{1,0:T(8,128)(2,1)S(1)} %get-tuple-element.14), channel_id=1, source_target_pairs={{0,1},{1,0},{2,3},{3,2},{4,5},{5,4},{6,7},{7,6},{8,9},{9,8},{10,11... | collective-permute-start | bytes 49160 | tf_op jit(solution)/shard_map/ppermute | solution.py:409
  21.0 5.8 %collective-permute-start.1 = (bf16[64,128]{1,0:T(8,128)(2,1)S(1)}, bf16[64,128]{1,0:T(8,128)(2,1)S(1)}, u32[]{:S(2)}, u32[]{:S(2)}) collective-permute-start(bf16[64,128]{1,0:T(8,128)(2,1)S(1)} %get-tuple-element.15), channel_id=1, source_target_pairs={{0,16},{1,2},{2,1},{3,4},{4,3},{5,6},{6,5},{7,8},{8,7},{9,10},{10,... | collective-permute-start | bytes 49160 | tf_op jit(solution)/shard_map/ppermute | solution.py:415
